TPU v7x, 512 devices: a whole 4x4x16 slice. The times are simulated.
512 devices in a mesh: strata: 128 (over z, x, core), comp: 4 (over y).
Axes of the slice: x: 4, y: 4, z: 16, core: 2. Of those that a mesh axis runs over, the one named last changes fastest.
Arguments:
- start_points: bfloat16 [2, 8, 2097152], P(None, None, 'strata'), may hold values from 0 to 1
- end_points: bfloat16 [2, 8, 2097152], P(None, None, 'strata'), may hold values from 0 to 1
- owner_lists: int32 [2, 16384, 1], P(None, 'strata'), may hold values from 0 to 127; in each aligned block of 128 rows (0 to 127, 128 to 255, ..., all dimensions but the last counted through in order) at most 2 rows name the same one
- local_strata: int32 [2, 16384], P(None, 'strata'), may hold values from 0 to 15
- last_coef: bfloat16 [2048, 64, 512], P('strata', 'comp'), may hold values from -6 to 6
- growth_rates: float32 [64], P('comp'), may hold values from 0.5 to 2
Outputs:
- middle_coef: bfloat16 [2048, 64, 512], P('strata', 'comp')
- first_coef: float32 [2048, 64, 512], P('strata', 'comp')
Inputs may be any that keep to these rules, and one draw needn't show every extreme that they name: `owner_lists`: in each step, among the 128 blocks of one index of strata no owner is named more than 2 times, a bound that some block reaches.
All inputs are finite; a program needn't handle non-finite values.
Results may differ from a plain program's by a relative error of at most 0.0075.
The roundings to bfloat16 on the way count: a program that leaves them out, or rounds other values in their place, can miss the bound.
Values may be sent and summed in bfloat16 or wider, within the bound.
A program may use at most 64 MiB of HBM per device.

v0:
```python
import jax
import jax.numpy as jnp
from jax import lax
from jax.sharding import PartitionSpec as P

COMPS = 64
BLOCK = 128
STEPS = 2
PATHS = 1024


root_three = 3.0**0.5
root_five = 5.0**0.5
root_seven = 7.0**0.5
step_length = 0.25


def sent_together(arrays, axis, split_dim, concat_dim, along):
    columns = [a.reshape(*a.shape[:along], -1) for a in arrays]
    both = jnp.concatenate(columns, axis=along)
    whole, at, finished = (
        lax.all_to_all(both, axis, split_axis=split_dim, concat_axis=concat_dim, tiled=True),
        0,
        [],
    )
    for a, column in zip(arrays, columns):
        section = whole[..., at : at + column.shape[along]]
        finished.append(section.reshape(*section.shape[:along], *a.shape[along:]))
        at += column.shape[along]
    return tuple(finished)


def sent_to_all(array, axis):
    peers = lax.axis_size(axis)
    return lax.all_to_all(
        jnp.broadcast_to(array[None], (peers, *array.shape)), axis, 0, 0, tiled=True
    )


def over_copies(array, axis):
    return sent_to_all(array, axis).sum(axis=0)


def legendre(columns):
    centered = 2.0 * columns[0] - 1.0
    features = jnp.stack(
        [
            jnp.ones_like(centered),
            root_three * centered,
            root_five * (1.5 * centered * centered - 0.5),
            root_seven * (2.5 * centered * centered * centered - 1.5 * centered),
        ],
        axis=-1,
    )
    for column in columns[1:]:
        factor = root_three * (2.0 * column - 1.0)
        features = jnp.concatenate([features, features * factor[..., None]], axis=-1)
    return (features * (1.0 / features.shape[-1] ** 0.5)).astype(jnp.bfloat16)


def evaluate(arrived, stratum_code, coeffs):
    block_count, dim_count, block_rows = arrived.shape
    strata_here, components_local, feature_count = coeffs.shape
    coefficient_rows = coeffs.reshape(strata_here, components_local * feature_count)
    strata_iota = jnp.arange(strata_here, dtype=jnp.int32)

    def compute_span(items):
        block_coords, span_codes = items
        features = legendre(
            [block_coords[:, index, :].astype(jnp.float32) for index in range(dim_count)]
        )
        choose_rows = (span_codes.astype(jnp.int32)[:, None] == strata_iota[None, :]).astype(
            jnp.bfloat16
        )
        picked = jnp.dot(choose_rows, coefficient_rows, preferred_element_type=jnp.float32).astype(
            jnp.bfloat16
        )
        picked = picked.reshape(choose_rows.shape[0], components_local, feature_count)
        return jnp.einsum(
            "brk,bck->bcr", features, picked, preferred_element_type=jnp.float32
        ).astype(jnp.bfloat16)

    def eval_span(items):
        return compute_span(items)

    spans = (
        arrived.reshape(block_count // 16, 16, dim_count, block_rows),
        stratum_code.reshape(block_count // 16, 16),
    )
    return lax.map(eval_span, spans).reshape(block_count, components_local, block_rows)


def per_device(start_points, end_points, owner_lists, local_strata, last_coef, growth_rates):
    n_owner = lax.axis_size("strata")
    dev_blocks = owner_lists.shape[1]
    capacity = max(2, (2 * dev_blocks + n_owner - 1) // n_owner)
    strata_here, components_local, feature_count = last_coef.shape
    dim_count = end_points.shape[1]
    block_rows = BLOCK
    blocks_per = PATHS // block_rows
    slot_total = n_owner * capacity
    block_iota = jnp.arange(dev_blocks, dtype=jnp.int32)
    slot_iota = jnp.arange(slot_total, dtype=jnp.int32)
    coeffs = last_coef
    middle = last_coef
    refitted = None
    for section in range(STEPS):
        owner_ids = owner_lists[section, :, 0]
        local_ids = local_strata[section]
        same_owner = (owner_ids[:, None] == owner_ids[None, :]) & (
            block_iota[None, :] < block_iota[:, None]
        )
        rank_in_pair = jnp.sum(same_owner.astype(jnp.int32), axis=1)
        slot_index = owner_ids * capacity + rank_in_pair
        placing = slot_index[None, :] == slot_iota[:, None]
        stratum_code = (
            (jnp.sum(jnp.where(placing, local_ids[None, :] + 1, 0), axis=1) - 1)
            .astype(jnp.bfloat16)
            .reshape(n_owner, capacity)
        )
        placing_bf = placing.astype(jnp.bfloat16)
        end_blocks = end_points[section].reshape(dim_count, dev_blocks, block_rows)
        packed = jnp.einsum(
            "sb,dbr->sdr", placing_bf, end_blocks, preferred_element_type=jnp.float32
        ).astype(jnp.bfloat16)
        packed = packed.reshape(n_owner, capacity, dim_count, block_rows)
        part_rows = block_rows // lax.axis_size("comp")
        comp_index = lax.axis_index("comp")
        sliced = lax.dynamic_slice_in_dim(packed, comp_index * part_rows, part_rows, 3)
        arrived, arrived_codes = sent_together((sliced, stratum_code), "strata", 0, 0, 2)
        arrived = lax.all_gather(arrived, "comp", axis=3, tiled=True)
        values = evaluate(
            arrived.reshape(slot_total, dim_count, block_rows),
            arrived_codes.reshape(slot_total),
            coeffs,
        )
        returned = lax.all_to_all(
            values.reshape(n_owner, capacity, components_local, block_rows),
            "strata",
            split_axis=0,
            concat_axis=0,
            tiled=True,
        )
        unpacked_values = jnp.einsum(
            "sb,scr->bcr",
            placing_bf,
            returned.reshape(slot_total, components_local, block_rows),
            preferred_element_type=jnp.float32,
        )
        local_square = jnp.sum(unpacked_values * unpacked_values, axis=1)
        mean_square = over_copies(local_square, "comp") / COMPS
        pressure = mean_square / (1.0 + mean_square)
        target = (
            unpacked_values
            + step_length
            * (
                growth_rates[None, :, None] * unpacked_values
                - unpacked_values * pressure[:, None, :]
            )
        ).astype(jnp.bfloat16)
        start_here = start_points[section]

        def stratum_projection(stratum, start_here=start_here, target=target):
            start_cols = lax.dynamic_slice_in_dim(start_here, stratum * PATHS, PATHS, 1)
            start_features = legendre(
                [start_cols[index].astype(jnp.float32) for index in range(dim_count)]
            )
            response_rows = lax.dynamic_slice_in_dim(target, stratum * blocks_per, blocks_per, 0)
            initial_rows = start_features.reshape(blocks_per, block_rows, feature_count)
            return jnp.einsum(
                "dza,dai->zi", response_rows, initial_rows, preferred_element_type=jnp.float32
            ) * (feature_count / PATHS)

        refitted = lax.map(stratum_projection, jnp.arange(strata_here, dtype=jnp.int32))
        if section == 0:
            middle = refitted.astype(jnp.bfloat16)
            coeffs = middle
    return (middle, refitted)


def solution(mesh):
    in_specs = (
        P(None, None, "strata"),
        P(None, None, "strata"),
        P(None, "strata", None),
        P(None, "strata"),
        P("strata", "comp", None),
        P("comp"),
    )
    out_specs = (P("strata", "comp", None), P("strata", "comp", None))
    return jax.shard_map(
        per_device, mesh=mesh, in_specs=in_specs, out_specs=out_specs, check_vma=False
    )
```

profile of v0, /device:TPU:32, one launch (start us, length us, event | category | flops | bytes accessed | tf_op | source)
XLA Modules:
  0.0 885.4 jit_solution(12165372198006185266)
XLA Ops:
  7.2 19.0 %all-to-all-start = ((bf16[128,2,257]{2,1,0:T(2,128)(2,1)}), bf16[128,2,257]{2,1,0:T(2,128)(2,1)S(1)}, u32[]{:S(2)}, u32[]{:S(2)}) async-start(bf16[128,2,257]{2,1,0:T(2,128)(2,1)} %copy.781), calls=%async_computation | async-start | bytes 393216 | tf_op jit(solution)/shard_map/all_to_all | solution.py:22
  27.9 18.1 %all-to-all-done = bf16[128,2,257]{2,1,0:T(2,128)(2,1)S(1)} async-done(((bf16[128,2,257]{2,1,0:T(2,128)(2,1)}), bf16[128,2,257]{2,1,0:T(2,128)(2,1)S(1)}, u32[]{:S(2)}, u32[]{:S(2)}) %all-to-all-start) | async-done | bytes 131616 | tf_op jit(solution)/shard_map/all_to_all | solution.py:22
  46.0 6.3 all-to-all-start.3
  52.6 13.3 %all_gather.6 = bf16[128,2,8,128]{0,2,1,3:T(8,128)(2,1)S(1)} all-gather(bf16[128,2,8,32]{0,2,1,3:T(8,128)(2,1)S(1)} %copy.783), channel_id=1, replica_groups=mesh['strata'=128,'comp'=4] {'comp'}, dimensions={3}, use_global_device_ids=true | all-gather | bytes 655360 | tf_op jit(solution)/shard_map/all_gather | solution.py:131
  67.1 38.7 %while.60 = (s32[]{:T(128)}, bf16[16,16,16,128]{3,2,1,0:T(8,128)(2,1)S(1)}, bf16[16,16]{1,0:T(8,128)(2,1)S(1)}, bf16[16,8192]{1,0:T(8,128)(2,1)S(1)}, bf16[16,16,8,128]{3,2,1,0:T(8,128)(2,1)S(1)}) while((s32[]{:T(128)}, bf16[16,16,16,128]{3,2,1,0:T(8,128)(2,1)S(1)}, bf16[16,16]{1,0:T(8,128)(2,1)S(1)}, ...), condition=%wide.region_3.4_spmd.clone.clone, body=%wide.region_2.3_spmd.clone.sunk.clone | while | flops 41246992 | bytes 22651116 | solution.py:90
  105.8 1.8 copy.786
  107.7 16.3 %all-to-all-start.1 = ((bf16[128,2,16,128]{3,1,2,0:T(2,128)(2,1)}), bf16[128,2,16,128]{3,1,2,0:T(2,128)(2,1)S(1)}, u32[]{:S(2)}, u32[]{:S(2)}) async-start(bf16[128,2,16,128]{3,1,2,0:T(2,128)(2,1)} %copy.786), calls=%async_computation.1 | async-start | bytes 2097152 | tf_op jit(solution)/shard_map/all_to_all | solution.py:137
  125.8 53.4 %all-to-all-done.1 = bf16[128,2,16,128]{3,1,2,0:T(2,128)(2,1)S(1)} async-done(((bf16[128,2,16,128]{3,1,2,0:T(2,128)(2,1)}), bf16[128,2,16,128]{3,1,2,0:T(2,128)(2,1)S(1)}, u32[]{:S(2)}, u32[]{:S(2)}) %all-to-all-start.1) | async-done | bytes 1048608 | tf_op jit(solution)/shard_map/all_to_all | solution.py:137
  181.3 4.0 all-to-all-start.2
  185.3 15.5 %all_gather.7 = bf16[128,2,8,128]{0,2,1,3:T(8,128)(2,1)S(1)} all-gather(bf16[128,2,8,32]{0,2,1,3:T(8,128)(2,1)S(1)} %copy.794), channel_id=1, replica_groups=mesh['strata'=128,'comp'=4] {'comp'}, dimensions={3}, use_global_device_ids=true | all-gather | bytes 655360 | tf_op jit(solution)/shard_map/all_gather | solution.py:131
  205.0 270.8 %while.58 = (s32[]{:T(128)}, bf16[16,16,512]{2,1,0:T(8,128)(2,1)}, s32[16]{0:T(128)}, bf16[128,16,128]{2,0,1:T(8,128)(2,1)}, bf16[8,16384]{1,0:T(8,128)(2,1)}, /*index=5*/s32[1]{0:T(128)}, s32[1]{0:T(128)}) while((s32[]{:T(128)}, bf16[16,16,512]{2,1,0:T(8,128)(2,1)}, s32[16]{0:T(128)}, bf16[128,16,128]{2,0,1:T(8,128)(2,1)}, ...), condition=%wide.region_7.8_spmd.clone, body=%wide.region_6.7_spmd.sunk.clone | while | flops 18964496 | bytes 23356412 | solution.py:174
  216.0 2.0 multiply_dynamic-update-slice_fusion.62
  232.9 2.0 multiply_dynamic-update-slice_fusion.62
  249.8 2.0 multiply_dynamic-update-slice_fusion.62
  266.7 2.0 multiply_dynamic-update-slice_fusion.62
  283.7 2.0 multiply_dynamic-update-slice_fusion.62
  300.6 2.0 multiply_dynamic-update-slice_fusion.62
  317.5 2.0 multiply_dynamic-update-slice_fusion.62
  334.4 2.0 multiply_dynamic-update-slice_fusion.62
  351.4 2.0 multiply_dynamic-update-slice_fusion.62
  368.3 2.0 multiply_dynamic-update-slice_fusion.62
  385.2 2.0 multiply_dynamic-update-slice_fusion.62
  402.1 2.0 multiply_dynamic-update-slice_fusion.62
  419.0 2.0 multiply_dynamic-update-slice_fusion.62
  436.0 2.0 multiply_dynamic-update-slice_fusion.62
  452.9 2.0 multiply_dynamic-update-slice_fusion.62
  469.8 2.0 multiply_dynamic-update-slice_fusion.62
  477.0 61.3 %while.61 = (s32[]{:T(128)}, bf16[16,16,16,128]{3,2,1,0:T(8,128)(2,1)S(1)}, bf16[16,16]{1,0:T(8,128)(2,1)}, bf16[16,8192]{1,0:T(8,128)(2,1)S(1)}, bf16[16,16,8,128]{3,2,1,0:T(8,128)(2,1)}) while((s32[]{:T(128)}, bf16[16,16,16,128]{3,2,1,0:T(8,128)(2,1)S(1)}, bf16[16,16]{1,0:T(8,128)(2,1)}, ...), condition=%wide.region_11.12_spmd.clone.clone, body=%wide.region_10.11_spmd.clone.sunk.clone | while | flops 41246992 | bytes 22651116 | solution.py:90
  539.2 61.6 %all_to_all.30 = bf16[128,2,16,128]{3,1,2,0:T(2,128)(2,1)S(1)} all-to-all(bf16[128,2,16,128]{3,1,2,0:T(2,128)(2,1)S(1)} %copy.797), channel_id=1, replica_groups=mesh['strata'=128,'comp'=4] {'strata'}, dimensions={0} | all-to-all | bytes 2097152 | tf_op jit(solution)/shard_map/all_to_all | solution.py:137
  602.9 3.4 all-to-all-start.5
  606.3 7.5 all-to-all-done.5
  615.5 269.8 %while.59 = (s32[]{:T(128)}, f32[16,16,512]{2,1,0:T(8,128)}, s32[16]{0:T(128)}, bf16[128,16,128]{2,0,1:T(8,128)(2,1)}, bf16[8,16384]{1,0:T(8,128)(2,1)}, /*index=5*/s32[1]{0:T(128)}, s32[1]{0:T(128)}) while((s32[]{:T(128)}, f32[16,16,512]{2,1,0:T(8,128)}, s32[16]{0:T(128)}, bf16[128,16,128]{2,0,1:T(8,128)(2,1)}, ...), condition=%wide.region_15.16_spmd.clone, body=%wide.region_14.15_spmd.sunk.clone | while | flops 18964496 | bytes 23356412 | solution.py:174
  626.5 2.0 multiply_dynamic-update-slice_fusion.65
  643.3 2.0 multiply_dynamic-update-slice_fusion.65
  660.2 2.0 multiply_dynamic-update-slice_fusion.65
  677.0 2.0 multiply_dynamic-update-slice_fusion.65
  693.9 2.0 multiply_dynamic-update-slice_fusion.65
  710.8 2.0 multiply_dynamic-update-slice_fusion.65
  727.6 2.0 multiply_dynamic-update-slice_fusion.65
  744.5 2.0 multiply_dynamic-update-slice_fusion.65
  761.3 2.0 multiply_dynamic-update-slice_fusion.65
  778.2 2.0 multiply_dynamic-update-slice_fusion.65
  795.1 2.0 multiply_dynamic-update-slice_fusion.65
  811.9 2.0 multiply_dynamic-update-slice_fusion.65
  828.8 2.0 multiply_dynamic-update-slice_fusion.65
  845.6 2.0 multiply_dynamic-update-slice_fusion.65
  862.5 2.0 multiply_dynamic-update-slice_fusion.65
  879.4 2.0 multiply_dynamic-update-slice_fusion.65
  (2824 shorter events, 546.3 us)
Async XLA Ops:
  3.4 2.5 copy-start.16
  3.4 2.4 copy-start.20
  4.3 21.9 %copy-start.15 = (bf16[16,16,512]{2,1,0:T(8,128)(2,1)S(1)}, bf16[16,16,512]{2,1,0:T(8,128)(2,1)}, u32[]{:S(2)}) copy-start(bf16[16,16,512]{2,1,0:T(8,128)(2,1)} %param.18) | copy-start | bytes 786436
  7.2 38.8 %all-to-all-start = ((bf16[128,2,257]{2,1,0:T(2,128)(2,1)}), bf16[128,2,257]{2,1,0:T(2,128)(2,1)S(1)}, u32[]{:S(2)}, u32[]{:S(2)}) async-start(bf16[128,2,257]{2,1,0:T(2,128)(2,1)} %copy.781), calls=%async_computation | async-start | bytes 393216 | tf_op jit(solution)/shard_map/all_to_all | solution.py:22
  46.0 61.7 %all-to-all-start.3 = ((bf16[128,2,257]{2,1,0:T(2,128)(2,1)}), bf16[128,2,257]{2,1,0:T(2,128)(2,1)S(1)}, u32[]{:S(2)}, u32[]{:S(2)}) async-start(bf16[128,2,257]{2,1,0:T(2,128)(2,1)} %copy.792), calls=%async_computation.3 | async-start | bytes 393216 | tf_op jit(solution)/shard_map/all_to_all | solution.py:22
  105.8 18.9 %copy-start.14 = (bf16[2,8,16384]{2,1,0:T(8,128)(2,1)S(1)}, bf16[2,8,16384]{2,1,0:T(8,128)(2,1)}, u32[]{:S(2)}) copy-start(bf16[2,8,16384]{2,1,0:T(8,128)(2,1)} %param.14) | copy-start | bytes 1572868
  107.7 71.6 %all-to-all-start.1 = ((bf16[128,2,16,128]{3,1,2,0:T(2,128)(2,1)}), bf16[128,2,16,128]{3,1,2,0:T(2,128)(2,1)S(1)}, u32[]{:S(2)}, u32[]{:S(2)}) async-start(bf16[128,2,16,128]{3,1,2,0:T(2,128)(2,1)} %copy.786), calls=%async_computation.1 | async-start | bytes 2097152 | tf_op jit(solution)/shard_map/all_to_all | solution.py:137
  180.6 22.8 %copy-start.18 = (f32[16]{0:T(128)S(1)}, f32[16]{0:T(128)}, u32[]{:S(2)}) copy-start(f32[16]{0:T(128)} %param.19) | copy-start | bytes 196
  181.3 22.0 %all-to-all-start.2 = ((f32[4,128,128]{2,1,0:T(8,128)}), f32[4,128,128]{2,1,0:T(8,128)S(1)}, u32[]{:S(2)}, u32[]{:S(2)}) async-start(f32[4,128,128]{2,1,0:T(8,128)} %broadcast_in_dim.84), calls=%async_computation.2 | async-start | bytes 524288 | tf_op jit(solution)/shard_map/all_to_all | solution.py:35
  214.2 0.9 copy-start.4
  214.2 1.0 copy-start.5
  231.1 0.9 copy-start.4
  231.1 1.0 copy-start.5
  248.1 0.9 copy-start.4
  248.1 1.0 copy-start.5
  265.0 0.9 copy-start.4
  265.0 1.0 copy-start.5
  281.9 1.0 copy-start.5
  298.8 1.0 copy-start.5
  315.8 1.0 copy-start.5
  332.7 1.0 copy-start.5
  349.6 1.0 copy-start.5
  366.5 1.0 copy-start.5
  383.4 1.0 copy-start.5
  400.4 1.0 copy-start.5
  417.3 1.0 copy-start.5
  434.2 1.0 copy-start.5
  451.1 1.0 copy-start.5
  468.1 1.0 copy-start.5
  539.2 62.6 %copy-start.17 = (s32[128]{0:T(128)S(1)}, s32[128]{0:T(128)}, u32[]{:S(2)}) copy-start(s32[128]{0:T(128)} %copy-done.16) | copy-start | bytes 1540
  601.8 12.1 %copy-start.19 = (f32[16]{0:T(128)S(1)}, f32[16]{0:T(128)}, u32[]{:S(2)}) copy-start(f32[16]{0:T(128)} %param.19) | copy-start | bytes 196
  602.9 10.9 %all-to-all-start.5 = ((f32[4,128,128]{2,1,0:T(8,128)}), f32[4,128,128]{2,1,0:T(8,128)S(1)}, u32[]{:S(2)}, u32[]{:S(2)}) async-start(f32[4,128,128]{2,1,0:T(8,128)} %broadcast_in_dim.87), calls=%async_computation.5 | async-start | bytes 524288 | tf_op jit(solution)/shard_map/all_to_all | solution.py:35
  624.7 1.0 copy-start.7
  641.6 1.0 copy-start.7
  658.4 1.0 copy-start.7
  675.3 1.0 copy-start.7
  692.1 1.0 copy-start.7
  709.0 1.0 copy-start.7
  725.9 1.0 copy-start.7
  742.7 1.0 copy-start.7
  759.6 1.0 copy-start.7
  776.4 1.0 copy-start.7
  793.3 1.0 copy-start.7
  810.2 1.0 copy-start.7
  827.0 1.0 copy-start.7
  843.9 1.0 copy-start.7
  860.7 1.0 copy-start.7
  877.7 1.0 copy-start.7
  (188 other events, 138.4 us)
where the time goes:
time: 900 us; the launch traced here: 885 us
  other arithmetic  301 us (33%)
  local copies, waits for them, and re-layouts  245 us (27%)
  blocking collectives  90.4 us (10%)
  waiting for transfers between devices  79 us (9%)
  matrix products  66 us (7%)
  loops' own time  54.3 us (6%)
  starting transfers between devices  49 us (5%)
    while x736, other arithmetic  134 us
    while x1120, local copies, waits for them, and re-layouts  122 us
    all_to_all x1, blocking collectives, per_device(): lax.all_to_all(values.reshape(n_owner, capacity, components_local, block_...  61.6 us
    mul x64, other arithmetic, legendre(): factor = root_three * (2.0 * column - 1.0)  54.4 us
    all_to_all x1, waiting for transfers between devices, per_device(): lax.all_to_all(values.reshape(n_owner, capacity, components_local, block_...  53.4 us
    concatenate x160, other arithmetic, legendre(): jnp.concatenate([features, features * factor[..., None]], axis=-1)  52.2 us
    another operation x2, loops' own time, per_device(): lax.map(stratum_projection, jnp.arange(strata_here, dtype=jnp.int32))  48.7 us
    dynamic_slice x32, local copies, waits for them, and re-layouts, per_device(): lax.map(stratum_projection, jnp.arange(strata_here, dtype=jnp.int32))  39.9 us
  transfers between devices with their start and end apart: 5, of which 3 were waited for; matrix products, arithmetic and copies ran while one was open for 5% of the time, Pallas kernels for 0%

commit v1 on v0

v1 whole, which is shorter than its diff:
```python
import math
import jax
import jax.numpy as jnp
from jax import lax
from jax.experimental import pallas as pl
from jax.experimental.pallas import tpu as pltpu
from jax.sharding import PartitionSpec as P

COMPS = 64
BLOCK = 128
STEPS = 2
PATHS = 1024
FEAT = 512

root_three = 3.0**0.5
root_five = 5.0**0.5
root_seven = 7.0**0.5
step_length = 0.25


def sent_together(arrays, axis, split_dim, concat_dim, along):
    columns = [a.reshape(*a.shape[:along], -1) for a in arrays]
    both = jnp.concatenate(columns, axis=along)
    whole, at, finished = (
        lax.all_to_all(both, axis, split_axis=split_dim, concat_axis=concat_dim, tiled=True),
        0,
        [],
    )
    for a, column in zip(arrays, columns):
        section = whole[..., at : at + column.shape[along]]
        finished.append(section.reshape(*section.shape[:along], *a.shape[along:]))
        at += column.shape[along]
    return tuple(finished)


def over_copies(array, axis):
    peers = lax.axis_size(axis)
    spread = lax.all_to_all(
        jnp.broadcast_to(array[None], (peers, *array.shape)), axis, 0, 0, tiled=True
    )
    return spread.sum(axis=0)


def feature_rows(points):
    centered = 2.0 * points - 1.0
    n = points.shape[1]
    row = lax.broadcasted_iota(jnp.int32, (8, n), 0)
    spread = [jnp.broadcast_to(centered[d : d + 1, :], (8, n)) for d in range(8)]
    x = spread[0]
    kind = row % 4
    scale = 1.0 / FEAT**0.5
    first = jnp.where(
        kind == 0,
        scale,
        jnp.where(
            kind == 1,
            (root_three * scale) * x,
            jnp.where(
                kind == 2,
                (root_five * scale) * (1.5 * x * x - 0.5),
                (root_seven * scale) * (2.5 * x * x * x - 1.5 * x),
            ),
        ),
    )
    first = jnp.where(row < 4, first, first * (root_three * spread[1]))
    columns = [first]
    for d in range(2, 8):
        factor = root_three * spread[d]
        columns = columns + [c * factor for c in columns]
    return jnp.concatenate(columns, axis=0).astype(jnp.bfloat16)


def evaluate_kernel(codes, points, coef, out):
    slots = points.shape[0]

    def pair(i, carry):
        a, b = 2 * i, 2 * i + 1
        u = jnp.concatenate([points[a], points[b]], axis=1).astype(jnp.float32)
        features = feature_rows(u)
        rows = jnp.concatenate([coef[codes[a]], coef[codes[b]]], axis=0)
        y = jnp.dot(rows, features, preferred_element_type=jnp.float32)
        c = y.shape[0] // 2
        out[a] = y[:c, :BLOCK].astype(jnp.bfloat16)
        out[b] = y[c:, BLOCK:].astype(jnp.bfloat16)
        return carry

    lax.fori_loop(0, slots // 2, pair, 0)


def evaluate(arrived, codes, coeffs):
    slots = arrived.shape[0]
    vmem = pl.BlockSpec(memory_space=pltpu.VMEM)
    return pl.pallas_call(
        evaluate_kernel,
        out_shape=jax.ShapeDtypeStruct((slots, coeffs.shape[1], BLOCK), jnp.bfloat16),
        in_specs=[pl.BlockSpec(memory_space=pltpu.SMEM), vmem, vmem],
        out_specs=vmem,
        name="evaluate",
    )(codes, arrived, coeffs)


def project_kernel(points, values, squares, rates, out, rounded):
    strata = out.shape[0]
    per = PATHS // BLOCK
    rate = rates[...]

    def one(q, carry):
        first = pl.multiple_of(q * PATHS, PATHS)
        targets = []
        for r in range(per):
            y = values[q * per + r].astype(jnp.float32)
            m = squares[pl.ds(q * per + r, 1), :] * (1.0 / COMPS)
            pressure = m / (1.0 + m)
            targets.append((y + step_length * (rate * y - y * pressure)).astype(jnp.bfloat16))
        acc = None
        for r in range(0, per, 2):
            u = points[:, pl.ds(first + r * BLOCK, 2 * BLOCK)].astype(jnp.float32)
            features = feature_rows(u)
            part = lax.dot_general(
                jnp.concatenate(targets[r : r + 2], axis=1),
                features,
                (((1,), (1,)), ((), ())),
                preferred_element_type=jnp.float32,
            )
            acc = part if acc is None else acc + part
        acc = acc * (FEAT / PATHS)
        out[q] = acc
        rounded[q] = acc.astype(jnp.bfloat16)
        return carry

    lax.fori_loop(0, strata, one, 0)


def project(points, values, squares, rates):
    strata = points.shape[1] // PATHS
    comps = values.shape[1]
    vmem = pl.BlockSpec(memory_space=pltpu.VMEM)
    return pl.pallas_call(
        project_kernel,
        out_shape=(
            jax.ShapeDtypeStruct((strata, comps, FEAT), jnp.float32),
            jax.ShapeDtypeStruct((strata, comps, FEAT), jnp.bfloat16),
        ),
        in_specs=[vmem] * 4,
        out_specs=(vmem, vmem),
        name="project",
    )(points, values, squares, rates)


def per_device(start_points, end_points, owner_lists, local_strata, last_coef, growth_rates):
    n_owner = lax.axis_size("strata")
    dev_blocks = owner_lists.shape[1]
    capacity = max(2, (2 * dev_blocks + n_owner - 1) // n_owner)
    components_local = last_coef.shape[1]
    dim_count = end_points.shape[1]
    slot_total = n_owner * capacity
    block_iota = jnp.arange(dev_blocks, dtype=jnp.int32)
    slot_iota = jnp.arange(slot_total, dtype=jnp.int32)
    rates = jnp.broadcast_to(growth_rates[:, None], (components_local, BLOCK))
    coeffs = last_coef
    middle = last_coef
    refitted = None
    for section in range(STEPS):
        owner_ids = owner_lists[section, :, 0]
        local_ids = local_strata[section]
        same_owner = (owner_ids[:, None] == owner_ids[None, :]) & (
            block_iota[None, :] < block_iota[:, None]
        )
        rank_in_pair = jnp.sum(same_owner.astype(jnp.int32), axis=1)
        slot_index = owner_ids * capacity + rank_in_pair
        placing = slot_index[None, :] == slot_iota[:, None]
        stratum_code = (
            jnp.sum(jnp.where(placing, local_ids[None, :], 0), axis=1)
            .astype(jnp.bfloat16)
            .reshape(n_owner, capacity)
        )
        placing_bf = placing.astype(jnp.bfloat16)
        end_blocks = end_points[section].reshape(dim_count, dev_blocks, BLOCK)
        packed = jnp.einsum(
            "sb,dbr->sdr", placing_bf, end_blocks, preferred_element_type=jnp.float32
        ).astype(jnp.bfloat16)
        packed = packed.reshape(n_owner, capacity, dim_count, BLOCK)
        part_rows = BLOCK // lax.axis_size("comp")
        comp_index = lax.axis_index("comp")
        sliced = lax.dynamic_slice_in_dim(packed, comp_index * part_rows, part_rows, 3)
        arrived, arrived_codes = sent_together((sliced, stratum_code), "strata", 0, 0, 2)
        arrived = lax.all_gather(arrived, "comp", axis=3, tiled=True)
        values = evaluate(
            arrived.reshape(slot_total, dim_count, BLOCK),
            arrived_codes.reshape(slot_total).astype(jnp.int32),
            coeffs,
        )
        returned = lax.all_to_all(
            values.reshape(n_owner, capacity, components_local, BLOCK),
            "strata",
            split_axis=0,
            concat_axis=0,
            tiled=True,
        )
        unpacked = jnp.einsum(
            "sb,scr->bcr",
            placing_bf,
            returned.reshape(slot_total, components_local, BLOCK),
            preferred_element_type=jnp.float32,
        )
        local_square = jnp.sum(unpacked * unpacked, axis=1)
        squares = over_copies(local_square, "comp")
        refitted, rounded = project(
            start_points[section], unpacked.astype(jnp.bfloat16), squares, rates
        )
        if section == 0:
            middle = rounded
            coeffs = middle
    return (middle, refitted)


def solution(mesh):
    in_specs = (
        P(None, None, "strata"),
        P(None, None, "strata"),
        P(None, "strata", None),
        P(None, "strata"),
        P("strata", "comp", None),
        P("comp"),
    )
    out_specs = (P("strata", "comp", None), P("strata", "comp", None))
    return jax.shard_map(
        per_device, mesh=mesh, in_specs=in_specs, out_specs=out_specs, check_vma=False
    )
```

time: 900 us -> 312 us (0.35)
  the two profiles are of different devices: /device:TPU:32 before, /device:TPU:1 now
where the time goes in v1:
time: 312 us; the launch traced here: 308 us
  blocking collectives  89.7 us (29%)
  waiting for transfers between devices  71.9 us (23%)
  Pallas kernels  65.9 us (21%)
  starting transfers between devices  53 us (17%)
  local copies, waits for them, and re-layouts  18.3 us (6%)
  other arithmetic  6.31 us (2%)
    all_to_all x1, blocking collectives, per_device(): lax.all_to_all(values.reshape(n_owner, capacity, components_local, BLOCK)...  66.1 us
    all_to_all x1, waiting for transfers between devices, per_device(): lax.all_to_all(values.reshape(n_owner, capacity, components_local, BLOCK)...  51 us
    pallas_call x2, Pallas kernels, evaluate(): pl.pallas_call(evaluate_kernel, out_shape=jax.ShapeDtypeStruct((slots, co...  48.7 us
    all_to_all x2, starting transfers between devices, sent_together(): lax.all_to_all(both, axis, split_axis=split_dim, concat_axis=concat_dim,...  28.4 us
    all_gather x2, blocking collectives, per_device(): arrived = lax.all_gather(arrived, 'comp', axis=3, tiled=True)  23.5 us
    all_to_all x1, starting transfers between devices, per_device(): lax.all_to_all(values.reshape(n_owner, capacity, components_local, BLOCK)...  17.5 us
    pallas_call x2, Pallas kernels, project(): pl.pallas_call(project_kernel, out_shape=(jax.ShapeDtypeStruct((strata, c...  17.3 us
    all_to_all x2, waiting for transfers between devices, sent_together(): lax.all_to_all(both, axis, split_axis=split_dim, concat_axis=concat_dim,...  16.5 us
  transfers between devices with their start and end apart: 5, of which 3 were waited for; matrix products, arithmetic and copies ran while one was open for 4% of the time, Pallas kernels for 8%

profile of v1, /device:TPU:1, one launch (start us, length us, event | category | flops | bytes accessed | tf_op | source)
XLA Modules:
  0.0 307.5 jit_solution(11185019268302891817)
XLA Ops:
  0.6 0.7 copy-done.1
  1.3 0.2 convert_reduce_fusion.2
  1.5 0.2 convert_reduce_fusion.3
  1.7 1.1 slice_bitcast_fusion
  2.8 0.4 convolution_convert_fusion
  3.2 0.4 convolution_convert_fusion.1
  3.6 1.2 constant_dynamic-slice_fusion
  4.8 0.4 copy.64
  5.2 0.3 copy-done.2
  5.6 0.2 convert_element_type.59
  5.9 0.8 copy.47
  6.8 20.4 %all-to-all-start = ((bf16[128,2,257]{2,1,0:T(2,128)(2,1)}), bf16[128,2,257]{2,1,0:T(2,128)(2,1)S(1)}, u32[]{:S(2)}, u32[]{:S(2)}) async-start(bf16[128,2,257]{2,1,0:T(2,128)(2,1)} %copy.47), calls=%async_computation | async-start | bytes 393216 | tf_op jit(solution)/shard_map/all_to_all | solution.py:25
  27.2 0.4 copy.66
  27.6 0.2 convert_element_type.66
  27.8 0.9 copy.55
  28.7 16.5 %all-to-all-done = bf16[128,2,257]{2,1,0:T(2,128)(2,1)S(1)} async-done(((bf16[128,2,257]{2,1,0:T(2,128)(2,1)}), bf16[128,2,257]{2,1,0:T(2,128)(2,1)S(1)}, u32[]{:S(2)}, u32[]{:S(2)}) %all-to-all-start) | async-done | bytes 131616 | tf_op jit(solution)/shard_map/all_to_all | solution.py:25
  45.2 8.0 %all-to-all-start.3 = ((bf16[128,2,257]{2,1,0:T(2,128)(2,1)}), bf16[128,2,257]{2,1,0:T(2,128)(2,1)S(1)}, u32[]{:S(2)}, u32[]{:S(2)}) async-start(bf16[128,2,257]{2,1,0:T(2,128)(2,1)} %copy.55), calls=%async_computation.3 | async-start | bytes 393216 | tf_op jit(solution)/shard_map/all_to_all | solution.py:25
  53.5 12.0 %all_gather.6 = bf16[128,2,8,128]{0,3,2,1:T(8,128)(2,1)S(1)} all-gather(bf16[128,2,8,32]{0,3,2,1:T(8,128)(2,1)S(1)} %bitcast.67), channel_id=1, replica_groups=mesh['strata'=128,'comp'=4] {'comp'}, dimensions={3}, use_global_device_ids=true | all-gather | bytes 655360 | tf_op jit(solution)/shard_map/all_gather | solution.py:187
  65.5 1.2 copy.49
  66.7 2.2 convert_reduce_fusion.1
  68.9 0.7 reshape.101.codes
  69.6 24.3 %evaluate.2 = bf16[256,16,128]{2,1,0:T(8,128)(2,1)} custom-call(s32[256]{0:T(256)} %reshape.101.codes, bf16[256,8,128]{2,1,0:T(8,128)(2,1)} %bitcast.63, bf16[16,16,512]{2,1,0:T(8,128)(2,1)} %coef.1), custom_call_target="tpu_custom_call" | custom-call | tf_op jit(solution)/shard_map/evaluate/pallas_call | solution.py:93
  94.0 17.5 %all-to-all-start.1 = ((bf16[128,2,16,128]{3,2,1,0:T(8,128)(2,1)}), bf16[128,2,16,128]{3,2,1,0:T(8,128)(2,1)S(1)}, u32[]{:S(2)}, u32[]{:S(2)}) async-start(bf16[128,2,16,128]{3,2,1,0:T(8,128)(2,1)} %bitcast.58), calls=%async_computation.1 | async-start | bytes 2097152 | tf_op jit(solution)/shard_map/all_to_all | solution.py:193
  111.5 0.8 slice_bitcast_fusion.1
  112.6 51.0 %all-to-all-done.1 = bf16[128,2,16,128]{3,2,1,0:T(8,128)(2,1)S(1)} async-done(((bf16[128,2,16,128]{3,2,1,0:T(8,128)(2,1)}), bf16[128,2,16,128]{3,2,1,0:T(8,128)(2,1)S(1)}, u32[]{:S(2)}, u32[]{:S(2)}) %all-to-all-start.1) | async-done | bytes 1048608 | tf_op jit(solution)/shard_map/all_to_all | solution.py:193
  163.6 1.0 copy.50
  164.6 0.4 multiply_reduce_fusion.1
  164.9 0.7 broadcast_in_dim.51
  165.7 3.7 %all-to-all-start.2 = ((f32[4,128,128]{2,1,0:T(8,128)}), f32[4,128,128]{2,1,0:T(8,128)S(1)}, u32[]{:S(2)}, u32[]{:S(2)}) async-start(f32[4,128,128]{2,1,0:T(8,128)} %broadcast_in_dim.51), calls=%async_computation.2 | async-start | bytes 524288 | tf_op jit(solution)/shard_map/all_to_all | solution.py:38
  169.4 11.5 %all_gather.7 = bf16[128,2,8,128]{0,3,2,1:T(8,128)(2,1)S(1)} all-gather(bf16[128,2,8,32]{0,3,2,1:T(8,128)(2,1)S(1)} %bitcast.64), channel_id=1, replica_groups=mesh['strata'=128,'comp'=4] {'comp'}, dimensions={3}, use_global_device_ids=true | all-gather | bytes 655360 | tf_op jit(solution)/shard_map/all_gather | solution.py:187
  180.9 1.2 copy.57
  182.1 2.2 convert_reduce_fusion
  184.3 0.7 reshape.102.codes
  185.1 1.1 copy.81.values
  186.2 0.6 reduce_sum.75.squares
  186.8 0.7 copy-done.3
  187.5 0.7 broadcast_in_dim.52.rates
  188.1 8.6 %project.2 = (f32[16,16,512]{2,1,0:T(8,128)}, bf16[16,16,512]{2,1,0:T(8,128)(2,1)}) custom-call(bf16[8,16384]{1,0:T(8,128)(2,1)} %get-tuple-element.9.points, bf16[128,16,128]{2,1,0:T(8,128)(2,1)} %copy.81.values, f32[128,128]{1,0:T(8,128)} %reduce_sum.75.squares, f32[16,128]{1,0:T(8,128)} %broadcast_in_dim.52.rates), custom_call_target="tpu_custom_call" | custom-call | tf_op jit(solution)/shard_map/project/pallas_call | solution.py:138
  196.8 24.3 %evaluate.3 = bf16[256,16,128]{2,1,0:T(8,128)(2,1)} custom-call(s32[256]{0:T(256)} %reshape.102.codes, bf16[256,8,128]{2,1,0:T(8,128)(2,1)} %bitcast.60, bf16[16,16,512]{2,1,0:T(8,128)(2,1)} %get-tuple-element.2.coef), custom_call_target="tpu_custom_call" | custom-call | tf_op jit(solution)/shard_map/evaluate/pallas_call | solution.py:93
  221.1 66.1 %all_to_all.30 = bf16[128,2,16,128]{3,2,1,0:T(8,128)(2,1)S(1)} all-to-all(bf16[128,2,16,128]{3,2,1,0:T(8,128)(2,1)} %bitcast.59), channel_id=1, replica_groups=mesh['strata'=128,'comp'=4] {'strata'}, dimensions={0} | all-to-all | bytes 2097152 | tf_op jit(solution)/shard_map/all_to_all | solution.py:193
  287.2 1.0 copy.58
  288.3 0.4 multiply_reduce_fusion
  288.6 0.7 broadcast_in_dim.55
  289.3 3.4 %all-to-all-start.5 = ((f32[4,128,128]{2,1,0:T(8,128)}), f32[4,128,128]{2,1,0:T(8,128)S(1)}, u32[]{:S(2)}, u32[]{:S(2)}) async-start(f32[4,128,128]{2,1,0:T(8,128)} %broadcast_in_dim.55), calls=%async_computation.5 | async-start | bytes 524288 | tf_op jit(solution)/shard_map/all_to_all | solution.py:38
  292.8 1.1 copy.80.values
  293.9 4.4 %all-to-all-done.5 = f32[4,128,128]{2,1,0:T(8,128)S(1)} async-done(((f32[4,128,128]{2,1,0:T(8,128)}), f32[4,128,128]{2,1,0:T(8,128)S(1)}, u32[]{:S(2)}, u32[]{:S(2)}) %all-to-all-start.5) | async-done | bytes 262176 | tf_op jit(solution)/shard_map/all_to_all | solution.py:38
  298.2 0.6 reduce_sum.79.squares
  298.9 8.6 %project.3 = (f32[16,16,512]{2,1,0:T(8,128)}, bf16[16,16,512]{2,1,0:T(8,128)(2,1)}) custom-call(bf16[8,16384]{1,0:T(8,128)(2,1)} %get-tuple-element.8.points, bf16[128,16,128]{2,1,0:T(8,128)(2,1)} %copy.80.values, f32[128,128]{1,0:T(8,128)} %reduce_sum.79.squares, f32[16,128]{1,0:T(8,128)} %broadcast_in_dim.52.rates), custom_call_target="tpu_custom_call" | custom-call | tf_op jit(solution)/shard_map/project/pallas_call | solution.py:138
  (21 shorter events, 0.9 us)
Async XLA Ops:
  0.6 0.7 copy-start.1
  4.8 0.7 copy-start.2
  6.8 38.4 %all-to-all-start = ((bf16[128,2,257]{2,1,0:T(2,128)(2,1)}), bf16[128,2,257]{2,1,0:T(2,128)(2,1)S(1)}, u32[]{:S(2)}, u32[]{:S(2)}) async-start(bf16[128,2,257]{2,1,0:T(2,128)(2,1)} %copy.47), calls=%async_computation | async-start | bytes 393216 | tf_op jit(solution)/shard_map/all_to_all | solution.py:25
  45.2 48.8 %all-to-all-start.3 = ((bf16[128,2,257]{2,1,0:T(2,128)(2,1)}), bf16[128,2,257]{2,1,0:T(2,128)(2,1)S(1)}, u32[]{:S(2)}, u32[]{:S(2)}) async-start(bf16[128,2,257]{2,1,0:T(2,128)(2,1)} %copy.55), calls=%async_computation.3 | async-start | bytes 393216 | tf_op jit(solution)/shard_map/all_to_all | solution.py:25
  94.0 17.5 %copy-start = (bf16[2,8,16384]{2,1,0:T(8,128)(2,1)S(1)}, bf16[2,8,16384]{2,1,0:T(8,128)(2,1)}, u32[]{:S(2)}) copy-start(bf16[2,8,16384]{2,1,0:T(8,128)(2,1)} %param.6) | copy-start | bytes 1572868
  94.0 69.6 %all-to-all-start.1 = ((bf16[128,2,16,128]{3,2,1,0:T(8,128)(2,1)}), bf16[128,2,16,128]{3,2,1,0:T(8,128)(2,1)S(1)}, u32[]{:S(2)}, u32[]{:S(2)}) async-start(bf16[128,2,16,128]{3,2,1,0:T(8,128)(2,1)} %bitcast.58), calls=%async_computation.1 | async-start | bytes 2097152 | tf_op jit(solution)/shard_map/all_to_all | solution.py:193
  165.7 20.5 %all-to-all-start.2 = ((f32[4,128,128]{2,1,0:T(8,128)}), f32[4,128,128]{2,1,0:T(8,128)S(1)}, u32[]{:S(2)}, u32[]{:S(2)}) async-start(f32[4,128,128]{2,1,0:T(8,128)} %broadcast_in_dim.51), calls=%async_computation.2 | async-start | bytes 524288 | tf_op jit(solution)/shard_map/all_to_all | solution.py:38
  186.8 0.7 copy-start.3
  289.3 8.9 %all-to-all-start.5 = ((f32[4,128,128]{2,1,0:T(8,128)}), f32[4,128,128]{2,1,0:T(8,128)S(1)}, u32[]{:S(2)}, u32[]{:S(2)}) async-start(f32[4,128,128]{2,1,0:T(8,128)} %broadcast_in_dim.55), calls=%async_computation.5 | async-start | bytes 524288 | tf_op jit(solution)/shard_map/all_to_all | solution.py:38

commit v2 on v1

v2 whole, which is shorter than its diff:
```python
import jax
import jax.numpy as jnp
from jax import lax
from jax.experimental import pallas as pl
from jax.experimental.pallas import tpu as pltpu
from jax.sharding import PartitionSpec as P

COMPS = 64
BLOCK = 128
STEPS = 2
PATHS = 1024
FEAT = 512
DIMS = 8
PLANES = 4
MESH = pl.DeviceIdType.MESH

root_three = 3.0**0.5
root_five = 5.0**0.5
root_seven = 7.0**0.5
step_length = 0.25


def plane_of(s):
    return lax.rem(s, 2) + 2 * lax.rem(s // 8 + lax.rem(s // 2, 4), 2)


def source_at(y, i):
    z = i // 2
    x = lax.rem(y // 2 + z, 2) + 2 * lax.rem(i, 2)
    return z * 8 + x * 2 + lax.rem(y, 2)


def turn(s, j, layers):
    k = j // 2
    m = k // 2 + 1
    dz = jnp.where(k == layers - 1, 0, jnp.where(lax.rem(k, 2) == 0, m, layers - m))
    z = lax.rem(s // 8 + dz, layers)
    return z * 2 + lax.rem(j + lax.rem(s // 2, 4) // 2, 2)


def feature_rows(points):
    centered = 2.0 * points - 1.0
    n = points.shape[1]
    row = lax.broadcasted_iota(jnp.int32, (8, n), 0)
    spread = [jnp.broadcast_to(centered[d : d + 1, :], (8, n)) for d in range(8)]
    x = spread[0]
    kind = row % 4
    scale = 1.0 / FEAT**0.5
    first = jnp.where(
        kind == 0,
        scale,
        jnp.where(
            kind == 1,
            (root_three * scale) * x,
            jnp.where(
                kind == 2,
                (root_five * scale) * (1.5 * x * x - 0.5),
                (root_seven * scale) * (2.5 * x * x * x - 1.5 * x),
            ),
        ),
    )
    first = jnp.where(row < 4, first, first * (root_three * spread[1]))
    columns = [first]
    for d in range(2, 8):
        factor = root_three * spread[d]
        columns = columns + [c * factor for c in columns]
    return jnp.concatenate(columns, axis=0).astype(jnp.bfloat16)


def remote(src, dst, ssem, rsem, device):
    return pltpu.make_async_remote_copy(
        src_ref=src,
        dst_ref=dst,
        send_sem=ssem,
        recv_sem=rsem,
        device_id=device,
        device_id_type=MESH,
    )


def drain(ref, sem):
    pltpu.make_async_copy(ref, ref, sem).wait()


def signal(barrier, device):
    pl.semaphore_signal(barrier, inc=1, device_id=device, device_id_type=MESH)


def send_or_keep(src, dst, ssem, rsem, device, mine):
    @pl.when(jnp.logical_not(mine))
    def _():
        remote(src, dst, ssem, rsem, device).start()

    @pl.when(mine)
    def _():
        pltpu.make_async_copy(src, dst, rsem).start()


def split_blocks(points, blocks):
    @pl.loop(0, blocks.shape[0])
    def _(b):
        blocks[b] = points[:, pl.ds(pl.multiple_of(b * BLOCK, BLOCK), BLOCK)]


def two_blocks(blocks, source, owner):
    return jnp.concatenate([blocks[source[2 * owner + r]] for r in range(2)], axis=0)


def exchange_kernel(
    source, points, table, coef, rates, coords, coef_all, rates_all, packed, blocks, s_p, r_p, s_c, r_c, s_r, r_r
):
    s = lax.axis_index("strata")
    y = lax.axis_index("comp")
    owners = packed.shape[0]
    layers = owners // 8
    members = coords.shape[0]
    own = plane_of(s) == y
    barrier = pltpu.get_barrier_semaphore()

    @pl.loop(0, members)
    def _(i):
        from_s = source_at(y, i)

        @pl.when(from_s != s)
        def _():
            signal(barrier, (from_s, y))

    for d in range(1, PLANES):
        signal(barrier, (s, lax.rem(y + d, PLANES)))

    @pl.when(own)
    def _():
        split_blocks(points, blocks)

        @pl.loop(0, owners)
        def _(o):
            packed[o, 0:16, :] = two_blocks(blocks, source, o)
            packed[o, 16:24, :] = table[...]

        pl.semaphore_wait(barrier, owners - 1 + PLANES - 1)

    @pl.when(jnp.logical_not(own))
    def _():
        pl.semaphore_wait(barrier, PLANES - 1)

    mine = (s // 8) * 2 + lax.rem(s // 2, 4) // 2

    @pl.when(own)
    def _():
        @pl.loop(0, owners)
        def _(j):
            k = j // 8
            m = k // 2 + 1
            dz = jnp.where(k == layers - 1, 0, jnp.where(lax.rem(k, 2) == 0, m, layers - m))
            o = lax.rem(s // 8 + dz, layers) * 8 + lax.rem(s + j, 8)
            send_or_keep(packed.at[o], coords.at[mine], s_p, r_p, (o, y), o == s)

    pltpu.make_async_copy(coef, coef_all.at[y], r_c).start()
    pltpu.make_async_copy(rates, rates_all.at[y], r_r).start()
    for d in range(1, PLANES):
        peer = (s, lax.rem(y + d, PLANES))
        remote(coef, coef_all.at[y], s_c, r_c, peer).start()
        remote(rates, rates_all.at[y], s_r, r_r, peer).start()

    drain(coords, r_p)
    drain(coef_all, r_c)
    drain(rates_all, r_r)
    drain(coef_all.at[pl.ds(0, PLANES - 1)], s_c)
    drain(rates_all.at[pl.ds(0, PLANES - 1)], s_r)

    @pl.when(own)
    def _():
        drain(packed.at[pl.ds(0, owners - 1)], s_p)


def main_kernel(
    codes,
    slots,
    source,
    coords,
    coef_all,
    rates,
    start,
    points,
    middle,
    first,
    feat_e,
    feat_p,
    send0,
    send1,
    recv0,
    recv1,
    coef1,
    packed,
    blocks,
    coords1,
    s_0,
    r_0,
    s_1,
    r_1,
    s_c,
    r_c,
    s_p,
    r_p,
):
    s = lax.axis_index("strata")
    y = lax.axis_index("comp")
    owners = packed.shape[0]
    layers = owners // 8
    members = coords.shape[0]
    strata_here = middle.shape[0]
    local = middle.shape[1]
    per = PATHS // BLOCK
    home = plane_of(s)
    own = home == y
    barrier = pltpu.get_barrier_semaphore()

    @pl.loop(0, owners)
    def _(o):
        @pl.when(jnp.logical_not((o == s) & own))
        def _():
            signal(barrier, (o, home))

    @pl.loop(0, members)
    def _(i):
        from_s = source_at(y, i)

        @pl.when(from_s != s)
        def _():
            signal(barrier, (from_s, y))

    for d in range(1, PLANES):
        signal(barrier, (s, lax.rem(y + d, PLANES)))

    def end_features(arrived):
        @pl.loop(0, members)
        def _(i):
            both = jnp.concatenate([arrived[i, 0:8, :], arrived[i, 8:16, :]], axis=1)
            feat_e[i] = feature_rows(both.astype(jnp.float32))

    def evaluate(i, step, coefs, send):
        for r in range(2):
            code = codes[step, 2 * i + r]
            rows = jnp.concatenate([coefs[c, code] for c in range(PLANES)], axis=0)
            value = jnp.dot(
                rows, feat_e[i, :, r * BLOCK : (r + 1) * BLOCK], preferred_element_type=jnp.float32
            )
            value = value.astype(jnp.bfloat16).astype(jnp.float32)
            square = jnp.sum(value * value, axis=0, keepdims=True) * (1.0 / COMPS)
            pressure = square / (1.0 + square)
            target = value + step_length * (rates[...] * value - value * pressure)
            target = target.astype(jnp.bfloat16)
            for c in range(PLANES):
                send[i, c, r] = target[c * local : (c + 1) * local]

    def give_back(i, send, recv, ssem, rsem):
        to = source_at(y, i)
        for c in range(PLANES):
            part = lax.rem(y + c, PLANES)
            send_or_keep(
                send.at[i, part],
                recv.at[pl.ds(2 * s, 2)],
                ssem,
                rsem,
                (to, part),
                (to == s) & (part == y),
            )

    def start_features(step):
        @pl.loop(0, strata_here * per // 2)
        def _(i):
            at = pl.multiple_of(i * (2 * BLOCK), 2 * BLOCK)
            feat_p[i] = feature_rows(start[step, :, pl.ds(at, 2 * BLOCK)].astype(jnp.float32))

    def refit(q, step, recv):
        acc = None
        for r in range(0, per, 2):
            both = jnp.concatenate(
                [recv[slots[step, q * per + r]], recv[slots[step, q * per + r + 1]]], axis=1
            )
            part = lax.dot_general(
                both,
                feat_p[q * (per // 2) + r // 2],
                (((1,), (1,)), ((), ())),
                preferred_element_type=jnp.float32,
            )
            acc = part if acc is None else acc + part
        return acc * (FEAT / PATHS)

    end_features(coords)

    @pl.loop(0, members)
    def _(i):
        evaluate(i, 0, coef_all, send0)

    @pl.when(own)
    def _():
        split_blocks(points, blocks)

        @pl.loop(0, owners)
        def _(o):
            packed[o] = two_blocks(blocks, source, o)

        pl.semaphore_wait(barrier, 2 * (owners - 1) + PLANES - 1)

    @pl.when(jnp.logical_not(own))
    def _():
        pl.semaphore_wait(barrier, members * PLANES + PLANES - 1)

    @pl.loop(0, members)
    def _(j):
        give_back(turn(s, j, layers), send0, recv0, s_0, r_0)

    mine = (s // 8) * 2 + lax.rem(s // 2, 4) // 2

    @pl.when(own)
    def _():
        @pl.loop(0, owners)
        def _(j):
            o = lax.rem(s + 1 + j, owners)
            send_or_keep(packed.at[o], coords1.at[mine], s_p, r_p, (o, y), o == s)

    start_features(0)
    drain(coords1, r_p)
    end_features(coords1)
    drain(recv0, r_0)

    def share(q):
        for d in range(1, PLANES):
            peer = (s, lax.rem(y + d, PLANES))
            remote(coef1.at[y, q], coef1.at[y, q], s_c, r_c, peer).start()

    @pl.loop(0, strata_here)
    def _(q):
        rounded = refit(q, 0, recv0).astype(jnp.bfloat16)
        middle[q] = rounded
        coef1[y, q] = rounded

        @pl.when(q > 0)
        def _():
            share(q - 1)

    share(strata_here - 1)
    drain(coef1.at[pl.ds(0, PLANES - 1)], r_c)

    @pl.loop(0, members)
    def _(j):
        evaluate(turn(s, j, layers), 1, coef1, send1)

        @pl.when(j > 0)
        def _():
            give_back(turn(s, j - 1, layers), send1, recv1, s_1, r_1)

    give_back(turn(s, members - 1, layers), send1, recv1, s_1, r_1)
    start_features(1)
    drain(recv1, r_1)

    @pl.loop(0, strata_here)
    def _(q):
        first[q] = refit(q, 1, recv1)

    drain(coef1.at[pl.ds(0, PLANES - 1)], s_c)

    @pl.when(own)
    def _():
        drain(packed.at[pl.ds(0, owners - 1)], s_p)
        drain(recv0.at[pl.ds(0, 2 * (owners - 1))], s_0)
        drain(recv1.at[pl.ds(0, 2 * (owners - 1))], s_1)

    @pl.when(jnp.logical_not(own))
    def _():
        drain(recv0, s_0)
        drain(recv1, s_1)


VMEM = pl.BlockSpec(memory_space=pltpu.VMEM)
SMEM = pl.BlockSpec(memory_space=pltpu.SMEM)
DMA = pltpu.SemaphoreType.DMA
LIMIT = 60 * 1024 * 1024


def exchange(source, points, table, coef, rates, owners):
    members = owners // PLANES
    strata_here, local, _ = coef.shape
    return pl.pallas_call(
        exchange_kernel,
        out_shape=(
            jax.ShapeDtypeStruct((members, 24, BLOCK), jnp.bfloat16),
            jax.ShapeDtypeStruct((PLANES, strata_here, local, FEAT), jnp.bfloat16),
            jax.ShapeDtypeStruct((PLANES, local, BLOCK), jnp.float32),
        ),
        in_specs=[SMEM, VMEM, VMEM, VMEM, VMEM],
        out_specs=(VMEM, VMEM, VMEM),
        scratch_shapes=[
            pltpu.VMEM((owners, 24, BLOCK), jnp.bfloat16),
            pltpu.VMEM((points.shape[1] // BLOCK, DIMS, BLOCK), jnp.bfloat16),
        ]
        + [DMA] * 6,
        compiler_params=pltpu.CompilerParams(
            collective_id=0, has_side_effects=True, vmem_limit_bytes=LIMIT
        ),
        name="exchange",
    )(source, points, table, coef, rates)


def main(codes, slots, source, coords, coef_all, rates, start, points, owners):
    members = owners // PLANES
    _, strata_here, local, _ = coef_all.shape
    bf = jnp.bfloat16
    return pl.pallas_call(
        main_kernel,
        out_shape=(
            jax.ShapeDtypeStruct((strata_here, local, FEAT), bf),
            jax.ShapeDtypeStruct((strata_here, local, FEAT), jnp.float32),
        ),
        in_specs=[SMEM] * 3 + [VMEM] * 5,
        out_specs=(VMEM, VMEM),
        scratch_shapes=[
            pltpu.VMEM((members, FEAT, 2 * BLOCK), bf),
            pltpu.VMEM((strata_here * PATHS // (2 * BLOCK), FEAT, 2 * BLOCK), bf),
            pltpu.VMEM((members, PLANES, 2, local, BLOCK), bf),
            pltpu.VMEM((members, PLANES, 2, local, BLOCK), bf),
            pltpu.VMEM((2 * owners, local, BLOCK), bf),
            pltpu.VMEM((2 * owners, local, BLOCK), bf),
            pltpu.VMEM((PLANES, strata_here, local, FEAT), bf),
            pltpu.VMEM((owners, 16, BLOCK), bf),
            pltpu.VMEM((points.shape[1] // BLOCK, DIMS, BLOCK), bf),
            pltpu.VMEM((members, 16, BLOCK), bf),
        ]
        + [DMA] * 8,
        compiler_params=pltpu.CompilerParams(
            collective_id=1, has_side_effects=True, vmem_limit_bytes=LIMIT
        ),
        name="steps",
    )(codes, slots, source, coords, coef_all, rates, start, points)


def per_device(start_points, end_points, owner_lists, local_strata, last_coef, growth_rates):
    owners = lax.axis_size("strata")
    dev_blocks = owner_lists.shape[1]
    local = last_coef.shape[1]
    me = lax.axis_index("strata")
    block_iota = jnp.arange(dev_blocks, dtype=jnp.int32)
    slot_iota = jnp.arange(2 * owners, dtype=jnp.int32)
    rates = jnp.broadcast_to(growth_rates[:, None], (local, BLOCK))

    owner_ids = owner_lists[:, :, 0]
    earlier = (owner_ids[:, :, None] == owner_ids[:, None, :]) & (
        block_iota[None, None, :] < block_iota[None, :, None]
    )
    slots = owner_ids * 2 + jnp.sum(earlier.astype(jnp.int32), axis=2)
    placing = slots[:, None, :] == slot_iota[None, :, None]
    source = jnp.sum(jnp.where(placing, block_iota[None, None, :], 0), axis=2)
    code = jnp.sum(jnp.where(placing, local_strata[:, None, :], 0), axis=2)
    table = code.reshape(STEPS, owners, 2).transpose(0, 2, 1).reshape(2 * STEPS, owners)
    table = jnp.pad(table, ((0, 8 - 2 * STEPS), (0, BLOCK - owners))).astype(jnp.bfloat16)

    coords, coef_all, rates_all = exchange(
        source[0], end_points[0], table, last_coef, rates, owners
    )
    here = jnp.arange(BLOCK, dtype=jnp.int32) == me
    arrived = coords[:, 16 : 16 + 2 * STEPS, :].astype(jnp.float32)
    codes = jnp.sum(jnp.where(here[None, None, :], arrived, 0.0), axis=2).astype(jnp.int32)
    codes = codes.reshape(-1, STEPS, 2).transpose(1, 0, 2).reshape(STEPS, -1)
    return main(
        codes,
        slots,
        source[1],
        coords,
        coef_all,
        rates_all.reshape(PLANES * local, BLOCK),
        start_points,
        end_points[1],
        owners,
    )


def solution(mesh):
    in_specs = (
        P(None, None, "strata"),
        P(None, None, "strata"),
        P(None, "strata", None),
        P(None, "strata"),
        P("strata", "comp", None),
        P("comp"),
    )
    out_specs = (P("strata", "comp", None), P("strata", "comp", None))
    return jax.shard_map(
        per_device, mesh=mesh, in_specs=in_specs, out_specs=out_specs, check_vma=False
    )
```

time: 312 us -> 194 us (0.62); the launches traced: 308 us -> 194 us
  Pallas kernels: 65.9 us -> 182 us
  blocking collectives: 89.7 us -> 0 us
  waiting for transfers between devices: 71.9 us -> 0 us
  starting transfers between devices: 53 us -> 0 us
  local copies, waits for them, and re-layouts: 18.3 us -> 9.69 us
  other arithmetic: 6.31 us -> 1.39 us
    pallas_call x4 -> x2, Pallas kernels: 65.9 us -> 182 us  [the longest x1 146 us: main(): pl.pallas_call(main_kernel, out_shape=(jax.ShapeDtypeStruct((strata_here,...]
    all_to_all x5 -> x0, waiting for transfers between devices: 71.9 us -> none  [the longest x1 51 us: per_device(): lax.all_to_all(values.reshape(n_owner, capacity, components_local, BLOCK)...]
    all_to_all x1 -> x0, blocking collectives: 66.1 us -> none  [per_device(): lax.all_to_all(values.reshape(n_owner, capacity, components_local, BLOCK)...]
    all_to_all x5 -> x0, starting transfers between devices: 53 us -> none  [the longest x2 28.4 us: sent_together(): lax.all_to_all(both, axis, split_axis=split_dim, concat_axis=concat_dim,...]
    all_gather x2 -> x0, blocking collectives: 23.5 us -> none  [per_device(): arrived = lax.all_gather(arrived, 'comp', axis=3, tiled=True)]
    convert_element_type x4 -> x1, other arithmetic: 4.47 us -> 0.01 us  [per_device(): jnp.sum(jnp.where(here[None, None, :], arrived, 0.0), axis=2)]
  transfers between devices with their start and end apart: 5 -> 0, of which waited for: 3 -> 0; matrix products, arithmetic and copies ran while one was open for 4% -> 0% of each run, Pallas kernels for 8% -> 0%
where the time goes in v2:
time: 194 us
  Pallas kernels  182 us (94%)
  local copies, waits for them, and re-layouts  9.69 us (5%)
    pallas_call x1, Pallas kernels, main(): pl.pallas_call(main_kernel, out_shape=(jax.ShapeDtypeStruct((strata_here,...  146 us
    pallas_call x1, Pallas kernels, exchange(): pl.pallas_call(exchange_kernel, out_shape=(jax.ShapeDtypeStruct((members,...  35.9 us
    unnamed x13, local copies, waits for them, and re-layouts  4.94 us

profile of v2, /device:TPU:1, one launch (start us, length us, event | category | flops | bytes accessed | tf_op | source)
XLA Modules:
  0.0 194.1 jit_solution(16688828448164161777)
XLA Ops:
  0.6 0.0 copy-start.4
  0.7 0.6 copy-done.4
  1.3 0.7 broadcast_in_dim.51.rates
  2.0 0.0 copy-start.2
  2.0 0.7 copy-done.2
  2.6 0.2 convert_reduce_fusion
  2.8 0.0 copy-start.3
  2.8 0.7 copy-done.3
  3.5 0.0 copy-start.1
  3.5 0.2 select_reduce_fusion
  3.7 0.4 copy-done.1
  4.1 0.6 fusion
  4.7 0.2 reshape.51
  4.9 0.1 copy.17
  5.0 0.6 pad.5.table
  5.6 1.9 slice_bitcast_fusion
  7.4 35.9 %exchange.1 = (bf16[32,24,128]{2,1,0:T(8,128)(2,1)}, bf16[4,16,16,512]{3,2,1,0:T(8,128)(2,1)}, f32[4,16,128]{2,1,0:T(8,128)}) custom-call(s32[256]{0:T(256)} %bitcast.20, bf16[8,16384]{1,0:T(8,128)(2,1)} %get-tuple-element.11.points, bf16[8,128]{1,0:T(8,128)(2,1)} %pad.5.table, bf16[16,16,512]{2,1,0:T(8,128)(2,1)} %coef.1, f32[16,128]{1,0:T(8,128)} %broadcast_in_dim.51.rates), custom_call_target="tpu_custom_call" | custom-call | tf_op jit(solution)/shard_map/exchange/pallas_call | solution.py:385
  43.3 0.9 select_reduce_fusion.2
  44.3 0.1 copy.20
  44.3 0.1 copy.19
  44.4 0.7 reshape.53.codes
  45.1 146.4 %steps.1 = (bf16[16,16,512]{2,1,0:T(8,128)(2,1)}, f32[16,16,512]{2,1,0:T(8,128)}) custom-call(s32[2,64]{1,0:T(2,128)} %reshape.53.codes, s32[2,128]{1,0:T(2,128)} %copy-done.1, s32[256]{0:T(256)} %bitcast.19, bf16[32,24,128]{2,1,0:T(8,128)(2,1)} %get-tuple-element.5.coords, bf16[4,16,16,512]{3,2,1,0:T(8,128)(2,1)} %get-tuple-element.6.coef_all, ...), custom_call_target="tpu_custom_call" | custom-call | tf_op jit(solution)/shard_map/steps/pallas_call | solution.py:410
  191.6 0.0 copy-start
  191.6 1.7 copy.23
  193.3 0.0 copy-done
  193.3 0.8 copy.24
  (5 shorter events, 0.0 us)
Async XLA Ops:
  0.6 0.7 copy-start.4
  2.0 0.7 copy-start.2
  2.8 0.7 copy-start.3
  3.5 0.6 copy-start.1
  191.6 1.7 copy-start

commit v3 on v2

--- a/solution.py
+++ b/solution.py
@@ -1,3 +1,5 @@
+import functools
+
 import jax
 import jax.numpy as jnp
 from jax import lax
@@ -12,6 +14,7 @@
 FEAT = 512
 DIMS = 8
 PLANES = 4
+ROOM = 4
 MESH = pl.DeviceIdType.MESH
 
 root_three = 3.0**0.5
@@ -30,12 +33,14 @@
     return z * 8 + x * 2 + lax.rem(y, 2)
 
 
-def turn(s, j, layers):
-    k = j // 2
+def layer_turn(s, k, layers):
     m = k // 2 + 1
     dz = jnp.where(k == layers - 1, 0, jnp.where(lax.rem(k, 2) == 0, m, layers - m))
-    z = lax.rem(s // 8 + dz, layers)
-    return z * 2 + lax.rem(j + lax.rem(s // 2, 4) // 2, 2)
+    return lax.rem(s // 8 + dz, layers)
+
+
+def turn(s, j, layers):
+    return layer_turn(s, j // 2, layers) * 2 + lax.rem(j + lax.rem(s // 2, 4) // 2, 2)
 
 
 def feature_rows(points):
@@ -96,10 +101,10 @@
         pltpu.make_async_copy(src, dst, rsem).start()
 
 
-def split_blocks(points, blocks):
+def split_blocks(points, step, blocks):
     @pl.loop(0, blocks.shape[0])
     def _(b):
-        blocks[b] = points[:, pl.ds(pl.multiple_of(b * BLOCK, BLOCK), BLOCK)]
+        blocks[b] = points[step, :, pl.ds(pl.multiple_of(b * BLOCK, BLOCK), BLOCK)]
 
 
 def two_blocks(blocks, source, owner):
@@ -107,7 +112,29 @@
 
 
 def exchange_kernel(
-    source, points, table, coef, rates, coords, coef_all, rates_all, packed, blocks, s_p, r_p, s_c, r_c, s_r, r_r
+    source,
+    points,
+    table,
+    coef,
+    rates,
+    coords,
+    coef_all,
+    rates_all,
+    tables,
+    full,
+    packed,
+    blocks,
+    flag,
+    s_p,
+    r_p,
+    s_c,
+    r_c,
+    s_r,
+    r_r,
+    s_t,
+    r_t,
+    s_f,
+    r_f,
 ):
     s = lax.axis_index("strata")
     y = lax.axis_index("comp")
@@ -125,23 +152,27 @@
         def _():
             signal(barrier, (from_s, y))
 
+    @pl.loop(1, layers)
+    def _(k):
+        signal(barrier, (lax.rem(s + 8 * k, owners), y))
+
     for d in range(1, PLANES):
         signal(barrier, (s, lax.rem(y + d, PLANES)))
 
     @pl.when(own)
     def _():
-        split_blocks(points, blocks)
+        split_blocks(points, 0, blocks)
 
         @pl.loop(0, owners)
         def _(o):
             packed[o, 0:16, :] = two_blocks(blocks, source, o)
             packed[o, 16:24, :] = table[...]
 
-        pl.semaphore_wait(barrier, owners - 1 + PLANES - 1)
+        pl.semaphore_wait(barrier, owners - 1 + layers - 1 + PLANES - 1)
 
     @pl.when(jnp.logical_not(own))
     def _():
-        pl.semaphore_wait(barrier, PLANES - 1)
+        pl.semaphore_wait(barrier, layers - 1 + PLANES - 1)
 
     mine = (s // 8) * 2 + lax.rem(s // 2, 4) // 2
 
@@ -149,11 +180,14 @@
     def _():
         @pl.loop(0, owners)
         def _(j):
-            k = j // 8
-            m = k // 2 + 1
-            dz = jnp.where(k == layers - 1, 0, jnp.where(lax.rem(k, 2) == 0, m, layers - m))
-            o = lax.rem(s // 8 + dz, layers) * 8 + lax.rem(s + j, 8)
+            o = layer_turn(s, j // 8, layers) * 8 + lax.rem(s + j, 8)
             send_or_keep(packed.at[o], coords.at[mine], s_p, r_p, (o, y), o == s)
+
+    pltpu.make_async_copy(table, tables.at[s // 8], r_t).start()
+
+    @pl.loop(1, layers)
+    def _(k):
+        remote(table, tables.at[s // 8], s_t, r_t, (lax.rem(s + 8 * k, owners), y)).start()
 
     pltpu.make_async_copy(coef, coef_all.at[y], r_c).start()
     pltpu.make_async_copy(rates, rates_all.at[y], r_r).start()
@@ -163,6 +197,17 @@
         remote(rates, rates_all.at[y], s_r, r_r, peer).start()
 
     drain(coords, r_p)
+    most = coords[0, 16:24, :].astype(jnp.float32)
+    for i in range(1, members):
+        most = jnp.maximum(most, coords[i, 16:24, :].astype(jnp.float32))
+    flag[...] = most
+    pltpu.make_async_copy(flag, full.at[y], r_f).start()
+    for d in range(1, PLANES):
+        remote(flag, full.at[y], s_f, r_f, (s, lax.rem(y + d, PLANES))).start()
+    drain(tables, r_t)
+    drain(tables.at[pl.ds(0, layers - 1)], s_t)
+    drain(full, r_f)
+    drain(full.at[pl.ds(0, PLANES - 1)], s_f)
     drain(coef_all, r_c)
     drain(rates_all, r_r)
     drain(coef_all.at[pl.ds(0, PLANES - 1)], s_c)
@@ -174,9 +219,11 @@
 
 
 def main_kernel(
+    room,
     codes,
     slots,
     source,
+    lists,
     coords,
     coef_all,
     rates,
@@ -186,18 +233,22 @@
     first,
     feat_e,
     feat_p,
-    send0,
-    send1,
+    sends,
+    seconds,
+    stage0,
+    stage1,
+    packs,
     recv0,
     recv1,
     coef1,
     packed,
     blocks,
     coords1,
-    s_0,
-    r_0,
-    s_1,
-    r_1,
+    s_v,
+    r_v,
+    s_w,
+    r_w,
+    s_z,
     s_c,
     r_c,
     s_p,
@@ -213,6 +264,11 @@
     per = PATHS // BLOCK
     home = plane_of(s)
     own = home == y
+    core = lax.rem(s, 2)
+    layer = s // 8
+    relay = core == lax.rem(y, 2)
+    stages = (stage0, stage1)
+    recvs = (recv0, recv1)
     barrier = pltpu.get_barrier_semaphore()
 
     @pl.loop(0, owners)
@@ -220,6 +276,19 @@
         @pl.when(jnp.logical_not((o == s) & own))
         def _():
             signal(barrier, (o, home))
+
+    @pl.loop(0, 16)
+    def _(j):
+        peer = layer * 8 + j // 2
+        plane = core + 2 * lax.rem(j, 2)
+
+        @pl.when(jnp.logical_not((peer == s) & (plane == y)))
+        def _():
+            signal(barrier, (peer, plane))
+
+    @pl.loop(1, layers)
+    def _(k):
+        signal(barrier, (lax.rem(s + 8 * k, owners), y))
 
     @pl.loop(0, members)
     def _(i):
@@ -238,7 +307,7 @@
             both = jnp.concatenate([arrived[i, 0:8, :], arrived[i, 8:16, :]], axis=1)
             feat_e[i] = feature_rows(both.astype(jnp.float32))
 
-    def evaluate(i, step, coefs, send):
+    def evaluate(i, step, coefs):
         for r in range(2):
             code = codes[step, 2 * i + r]
             rows = jnp.concatenate([coefs[c, code] for c in range(PLANES)], axis=0)
@@ -251,19 +320,53 @@
             target = value + step_length * (rates[...] * value - value * pressure)
             target = target.astype(jnp.bfloat16)
             for c in range(PLANES):
-                send[i, c, r] = target[c * local : (c + 1) * local]
-
-    def give_back(i, send, recv, ssem, rsem):
+                (seconds if r else sends)[step, i, c] = target[c * local : (c + 1) * local]
+
+    def give_first(i, step):
         to = source_at(y, i)
         for c in range(PLANES):
             part = lax.rem(y + c, PLANES)
             send_or_keep(
-                send.at[i, part],
-                recv.at[pl.ds(2 * s, 2)],
-                ssem,
-                rsem,
+                sends.at[step, i, part],
+                recvs[step].at[s],
+                s_v.at[step],
+                r_v.at[step],
                 (to, part),
                 (to == s) & (part == y),
+            )
+
+    def give_second(i, step):
+        source_of = source_at(y, i)
+        to = layer * 8 + lax.rem(source_of, 8)
+        for c in range(PLANES):
+            part = lax.rem(y + c, PLANES)
+            send_or_keep(
+                seconds.at[step, i, part],
+                stages[step].at[source_of // 8, lax.rem(s, 8)],
+                s_w.at[step],
+                r_w.at[step],
+                (to, part),
+                (to == s) & (part == y),
+            )
+
+    def pass_on(step):
+        drain(stages[step], r_w.at[step])
+
+        @pl.loop(0, layers)
+        def _(z):
+            for k in range(room):
+                packs[step, z, k] = stages[step][z, lists[step, z * 8 + k]]
+
+        @pl.loop(0, layers)
+        def _(k):
+            z = layer_turn(s, k, layers)
+            send_or_keep(
+                packs.at[step, z],
+                recvs[step].at[pl.ds(owners + layer * room, room)],
+                s_z.at[step],
+                r_v.at[step],
+                (z * 8 + lax.rem(s, 8), y),
+                z == layer,
             )
 
     def start_features(step):
@@ -272,11 +375,11 @@
             at = pl.multiple_of(i * (2 * BLOCK), 2 * BLOCK)
             feat_p[i] = feature_rows(start[step, :, pl.ds(at, 2 * BLOCK)].astype(jnp.float32))
 
-    def refit(q, step, recv):
+    def refit(q, step):
         acc = None
         for r in range(0, per, 2):
             both = jnp.concatenate(
-                [recv[slots[step, q * per + r]], recv[slots[step, q * per + r + 1]]], axis=1
+                [recvs[step][slots[step, q * per + r + h]] for h in range(2)], axis=1
             )
             part = lax.dot_general(
                 both,
@@ -291,25 +394,33 @@
 
     @pl.loop(0, members)
     def _(i):
-        evaluate(i, 0, coef_all, send0)
+        evaluate(i, 0, coef_all)
 
     @pl.when(own)
     def _():
-        split_blocks(points, blocks)
+        split_blocks(points, 1, blocks)
 
         @pl.loop(0, owners)
         def _(o):
             packed[o] = two_blocks(blocks, source, o)
 
-        pl.semaphore_wait(barrier, 2 * (owners - 1) + PLANES - 1)
-
-    @pl.when(jnp.logical_not(own))
-    def _():
-        pl.semaphore_wait(barrier, members * PLANES + PLANES - 1)
+        pl.semaphore_wait(barrier, 2 * (owners - 1) + 15 + layers - 1 + PLANES - 1)
+
+    @pl.when(relay & jnp.logical_not(own))
+    def _():
+        pl.semaphore_wait(barrier, owners + 15 + layers - 1 + PLANES - 1)
+
+    @pl.when(jnp.logical_not(relay))
+    def _():
+        pl.semaphore_wait(barrier, owners + 16 + layers - 1 + PLANES - 1)
 
     @pl.loop(0, members)
     def _(j):
-        give_back(turn(s, j, layers), send0, recv0, s_0, r_0)
+        give_second(turn(s, j, layers), 0)
+
+    @pl.loop(0, members)
+    def _(j):
+        give_first(turn(s, j, layers), 0)
 
     mine = (s // 8) * 2 + lax.rem(s // 2, 4) // 2
 
@@ -320,10 +431,11 @@
             o = lax.rem(s + 1 + j, owners)
             send_or_keep(packed.at[o], coords1.at[mine], s_p, r_p, (o, y), o == s)
 
+    pass_on(0)
     start_features(0)
     drain(coords1, r_p)
     end_features(coords1)
-    drain(recv0, r_0)
+    drain(recv0, r_v.at[0])
 
     def share(q):
         for d in range(1, PLANES):
@@ -332,7 +444,7 @@
 
     @pl.loop(0, strata_here)
     def _(q):
-        rounded = refit(q, 0, recv0).astype(jnp.bfloat16)
+        rounded = refit(q, 0).astype(jnp.bfloat16)
         middle[q] = rounded
         coef1[y, q] = rounded
 
@@ -345,32 +457,47 @@
 
     @pl.loop(0, members)
     def _(j):
-        evaluate(turn(s, j, layers), 1, coef1, send1)
+        evaluate(turn(s, j, layers), 1, coef1)
 
         @pl.when(j > 0)
         def _():
-            give_back(turn(s, j - 1, layers), send1, recv1, s_1, r_1)
-
-    give_back(turn(s, members - 1, layers), send1, recv1, s_1, r_1)
+            give_second(turn(s, j - 1, layers), 1)
+            give_first(turn(s, j - 1, layers), 1)
+
+    give_second(turn(s, members - 1, layers), 1)
+    give_first(turn(s, members - 1, layers), 1)
+    pass_on(1)
     start_features(1)
-    drain(recv1, r_1)
+    drain(recv1, r_v.at[1])
 
     @pl.loop(0, strata_here)
     def _(q):
-        first[q] = refit(q, 1, recv1)
+        first[q] = refit(q, 1)
 
     drain(coef1.at[pl.ds(0, PLANES - 1)], s_c)
 
+    for step in range(STEPS):
+        drain(packs.at[step, pl.ds(0, layers - 1)], s_z.at[step])
+
+        @pl.when(own)
+        def _():
+            drain(recvs[step].at[pl.ds(0, owners - 1)], s_v.at[step])
+
+        @pl.when(jnp.logical_not(own))
+        def _():
+            drain(recvs[step].at[pl.ds(0, owners)], s_v.at[step])
+
+        @pl.when(relay)
+        def _():
+            drain(recvs[step].at[pl.ds(0, owners - layers // 2)], s_w.at[step])
+
+        @pl.when(jnp.logical_not(relay))
+        def _():
+            drain(recvs[step].at[pl.ds(0, owners)], s_w.at[step])
+
     @pl.when(own)
     def _():
         drain(packed.at[pl.ds(0, owners - 1)], s_p)
-        drain(recv0.at[pl.ds(0, 2 * (owners - 1))], s_0)
-        drain(recv1.at[pl.ds(0, 2 * (owners - 1))], s_1)
-
-    @pl.when(jnp.logical_not(own))
-    def _():
-        drain(recv0, s_0)
-        drain(recv1, s_1)
 
 
 VMEM = pl.BlockSpec(memory_space=pltpu.VMEM)
@@ -388,14 +515,17 @@
             jax.ShapeDtypeStruct((members, 24, BLOCK), jnp.bfloat16),
             jax.ShapeDtypeStruct((PLANES, strata_here, local, FEAT), jnp.bfloat16),
             jax.ShapeDtypeStruct((PLANES, local, BLOCK), jnp.float32),
+            jax.ShapeDtypeStruct((owners // 8, 8, BLOCK), jnp.bfloat16),
+            jax.ShapeDtypeStruct((PLANES, 8, BLOCK), jnp.float32),
         ),
         in_specs=[SMEM, VMEM, VMEM, VMEM, VMEM],
-        out_specs=(VMEM, VMEM, VMEM),
+        out_specs=(VMEM,) * 5,
         scratch_shapes=[
             pltpu.VMEM((owners, 24, BLOCK), jnp.bfloat16),
-            pltpu.VMEM((points.shape[1] // BLOCK, DIMS, BLOCK), jnp.bfloat16),
+            pltpu.VMEM((points.shape[2] // BLOCK, DIMS, BLOCK), jnp.bfloat16),
+            pltpu.VMEM((8, BLOCK), jnp.float32),
         ]
-        + [DMA] * 6,
+        + [DMA] * 10,
         compiler_params=pltpu.CompilerParams(
             collective_id=0, has_side_effects=True, vmem_limit_bytes=LIMIT
         ),
@@ -403,36 +533,41 @@
     )(source, points, table, coef, rates)
 
 
-def main(codes, slots, source, coords, coef_all, rates, start, points, owners):
+def main(room, codes, slots, source, lists, coords, coef_all, rates, start, points, owners):
+    layers = owners // 8
     members = owners // PLANES
     _, strata_here, local, _ = coef_all.shape
     bf = jnp.bfloat16
     return pl.pallas_call(
-        main_kernel,
+        functools.partial(main_kernel, room),
         out_shape=(
             jax.ShapeDtypeStruct((strata_here, local, FEAT), bf),
             jax.ShapeDtypeStruct((strata_here, local, FEAT), jnp.float32),
         ),
-        in_specs=[SMEM] * 3 + [VMEM] * 5,
+        in_specs=[SMEM] * 4 + [VMEM] * 5,
         out_specs=(VMEM, VMEM),
         scratch_shapes=[
             pltpu.VMEM((members, FEAT, 2 * BLOCK), bf),
             pltpu.VMEM((strata_here * PATHS // (2 * BLOCK), FEAT, 2 * BLOCK), bf),
-            pltpu.VMEM((members, PLANES, 2, local, BLOCK), bf),
-            pltpu.VMEM((members, PLANES, 2, local, BLOCK), bf),
-            pltpu.VMEM((2 * owners, local, BLOCK), bf),
-            pltpu.VMEM((2 * owners, local, BLOCK), bf),
+            pltpu.VMEM((STEPS, members, PLANES, local, BLOCK), bf),
+            pltpu.VMEM((STEPS, members, PLANES, local, BLOCK), bf),
+            pltpu.VMEM((layers, 8, local, BLOCK), bf),
+            pltpu.VMEM((layers, 8, local, BLOCK), bf),
+            pltpu.VMEM((STEPS, layers, room, local, BLOCK), bf),
+            pltpu.VMEM((owners + layers * room, local, BLOCK), bf),
+            pltpu.VMEM((owners + layers * room, local, BLOCK), bf),
             pltpu.VMEM((PLANES, strata_here, local, FEAT), bf),
             pltpu.VMEM((owners, 16, BLOCK), bf),
-            pltpu.VMEM((points.shape[1] // BLOCK, DIMS, BLOCK), bf),
+            pltpu.VMEM((points.shape[2] // BLOCK, DIMS, BLOCK), bf),
             pltpu.VMEM((members, 16, BLOCK), bf),
         ]
-        + [DMA] * 8,
+        + [DMA((STEPS,))] * 5
+        + [DMA] * 4,
         compiler_params=pltpu.CompilerParams(
-            collective_id=1, has_side_effects=True, vmem_limit_bytes=LIMIT
+            collective_id=room, has_side_effects=True, vmem_limit_bytes=LIMIT
         ),
         name="steps",
-    )(codes, slots, source, coords, coef_all, rates, start, points)
+    )(codes, slots, source, lists, coords, coef_all, rates, start, points)
 
 
 def per_device(start_points, end_points, owner_lists, local_strata, last_coef, growth_rates):
@@ -444,35 +579,63 @@
     slot_iota = jnp.arange(2 * owners, dtype=jnp.int32)
     rates = jnp.broadcast_to(growth_rates[:, None], (local, BLOCK))
 
+    layers = owners // 8
     owner_ids = owner_lists[:, :, 0]
     earlier = (owner_ids[:, :, None] == owner_ids[:, None, :]) & (
         block_iota[None, None, :] < block_iota[None, :, None]
     )
-    slots = owner_ids * 2 + jnp.sum(earlier.astype(jnp.int32), axis=2)
+    second = jnp.sum(earlier.astype(jnp.int32), axis=2)
+    slots = owner_ids * 2 + second
     placing = slots[:, None, :] == slot_iota[None, :, None]
     source = jnp.sum(jnp.where(placing, block_iota[None, None, :], 0), axis=2)
     code = jnp.sum(jnp.where(placing, local_strata[:, None, :], 0), axis=2)
+    ahead = (
+        (second[:, None, :] == 1)
+        & (owner_ids[:, :, None] // 8 == owner_ids[:, None, :] // 8)
+        & (owner_ids[:, None, :] < owner_ids[:, :, None])
+    )
+    place = jnp.sum(ahead.astype(jnp.int32), axis=2)
+    entry = jnp.where(second == 1, owner_ids // 8 * 8 + place, -1)
+    listing = entry[:, None, :] == jnp.arange(owners, dtype=jnp.int32)[None, :, None]
+    lists = jnp.sum(jnp.where(listing, owner_ids[:, None, :] % 8, 0), axis=2)
+    over = jnp.max(jnp.where(second == 1, place, 0)) >= ROOM
     table = code.reshape(STEPS, owners, 2).transpose(0, 2, 1).reshape(2 * STEPS, owners)
-    table = jnp.pad(table, ((0, 8 - 2 * STEPS), (0, BLOCK - owners))).astype(jnp.bfloat16)
-
-    coords, coef_all, rates_all = exchange(
-        source[0], end_points[0], table, last_coef, rates, owners
+    table = jnp.concatenate(
+        [table, lists, jnp.broadcast_to(over.astype(jnp.int32), (2, owners))], axis=0
+    )
+    table = jnp.pad(table, ((0, 0), (0, BLOCK - owners))).astype(jnp.bfloat16)
+
+    coords, coef_all, rates_all, tables, full = exchange(
+        source[0], end_points, table, last_coef, rates, owners
     )
     here = jnp.arange(BLOCK, dtype=jnp.int32) == me
     arrived = coords[:, 16 : 16 + 2 * STEPS, :].astype(jnp.float32)
     codes = jnp.sum(jnp.where(here[None, None, :], arrived, 0.0), axis=2).astype(jnp.int32)
     codes = codes.reshape(-1, STEPS, 2).transpose(1, 0, 2).reshape(STEPS, -1)
-    return main(
-        codes,
-        slots,
-        source[1],
-        coords,
-        coef_all,
-        rates_all.reshape(PLANES * local, BLOCK),
-        start_points,
-        end_points[1],
-        owners,
-    )
+    wanted = tables[:, 2 * STEPS : 3 * STEPS, :owners].astype(jnp.float32)
+    wanted = wanted.reshape(layers, STEPS, layers, 8)
+    at_layer = jnp.arange(layers, dtype=jnp.int32) == me // 8
+    wanted = jnp.sum(jnp.where(at_layer[None, None, :, None], wanted, 0.0), axis=2)
+    wanted = wanted.astype(jnp.int32).transpose(1, 0, 2).reshape(STEPS, layers * 8)
+    crowded = jnp.max(full[:, 3 * STEPS, :]) > 0.5
+
+    def run(room):
+        index = jnp.where(second == 1, owners + owner_ids // 8 * room + place, owner_ids)
+        return main(
+            room,
+            codes,
+            index,
+            source[1],
+            wanted,
+            coords,
+            coef_all,
+            rates_all.reshape(PLANES * local, BLOCK),
+            start_points,
+            end_points,
+            owners,
+        )
+
+    return lax.cond(crowded, lambda: run(8), lambda: run(ROOM))
 
 
 def solution(mesh):

time: 194 us -> 177 us (0.912)
  Pallas kernels: 182 us -> 162 us
  other arithmetic: 1.39 us -> 4.98 us
  local copies, waits for them, and re-layouts: 9.69 us -> 7.27 us
    pallas_call x1, Pallas kernels: 146 us -> 122 us  [main(): pl.pallas_call(functools.partial(main_kernel, room), out_shape=(jax.Shape...]
    pallas_call x1, Pallas kernels: 35.9 us -> 40.2 us  [exchange(): pl.pallas_call(exchange_kernel, out_shape=(jax.ShapeDtypeStruct((members,...]
    reduce_max x0 -> x2, other arithmetic: none -> 1.97 us  [the longest x1 1.33 us: per_device(): crowded = jnp.max(full[:, 3 * STEPS, :]) > 0.5]
where the time goes in v3:
time: 177 us; the launch traced here: 176 us
  Pallas kernels  162 us (92%)
  local copies, waits for them, and re-layouts  7.27 us (4%)
  other arithmetic  4.98 us (3%)
  between operations  2.11 us (1%)
    pallas_call x1, Pallas kernels, main(): pl.pallas_call(functools.partial(main_kernel, room), out_shape=(jax.Shape...  122 us
    pallas_call x1, Pallas kernels, exchange(): pl.pallas_call(exchange_kernel, out_shape=(jax.ShapeDtypeStruct((members,...  40.2 us

profile of v3, /device:TPU:1, one launch (start us, length us, event | category | flops | bytes accessed | tf_op | source)
XLA Modules:
  0.0 176.3 jit_solution(4843450927782958102)
XLA Ops:
  0.7 0.0 copy-start.2
  0.7 0.7 copy-done.2
  1.3 0.0 copy-start.4
  1.4 0.6 copy-done.4
  2.0 0.7 broadcast_in_dim.87.rates
  2.7 0.2 convert_reduce_fusion.1
  2.9 0.2 convert_reduce_fusion
  3.1 0.6 select_reduce_fusion.4
  4.4 0.1 select_reduce_fusion.2
  4.5 0.0 copy-start.3
  4.6 0.1 pad.2.clone
  4.6 0.6 copy-done.3
  5.2 0.2 select_reduce_fusion
  5.5 0.6 slice.22
  6.0 0.2 reshape.174
  6.2 0.1 copy.34
  6.3 0.7 maximum_maximum_fusion.table
  7.0 0.0 copy-start
  7.0 0.0 copy-start.1
  7.0 40.2 %exchange.1 = (bf16[32,24,128]{2,1,0:T(8,128)(2,1)S(1)}, bf16[4,16,16,512]{3,2,1,0:T(8,128)(2,1)S(1)}, f32[4,16,128]{2,1,0:T(8,128)S(1)}, bf16[16,8,128]{2,1,0:T(8,128)(2,1)}, f32[4,8,128]{2,1,0:T(8,128)}) custom-call(s32[256]{0:T(256)} %bitcast.28, bf16[2,8,16384]{2,1,0:T(8,128)(2,1)} %points.1, bf16[8,128]{1,0:T(8,128)(2,1)} %maximum_maximum_fusion.table, ...), custom_call_target="tpu_custom_call" | custom-call | tf_op jit(solution)/shard_map/exchange/pallas_call | solution.py:512
  47.2 1.3 slice_reduce_fusion
  49.1 0.1 select_reduce_fusion.3
  49.3 0.1 copy.41
  49.4 0.8 slice_convert_fusion
  50.1 0.1 copy.36
  50.2 0.1 fusion
  50.3 0.0 copy-done
  50.3 0.0 copy-done.1
  50.4 124.4 %conditional.1 = ((bf16[16,16,512]{2,1,0:T(8,128)(2,1)S(1)}, f32[16,16,512]{2,1,0:T(8,128)S(1)})) conditional(s32[]{:T(128)} %convert_element_type.34, (s32[2,128]{1,0:T(2,128)S(1)}, s32[2,128]{1,0:T(2,128)S(1)}, s32[2,128]{1,0:T(2,128)S(1)}, s32[2,256]{1,0:T(2,128)S(1)}, f32[4,16,128]{2,1,0:T(8,128)S(1)}, /*index=5*/s32[2,32,2]{1,2,0:T(2,128)S(1)}, ...), branch_computations={%region_9.10_spmd, %region_10.11_spmd} | conditional | flops 5120 | bytes 12296 | solution.py:638
  50.4 0.6 slice.12
  51.0 0.6 compare_select_fusion.slots
  51.5 0.1 copy.38
  51.6 0.7 reshape.182.lists
  52.3 0.1 copy.37
  52.4 0.7 reshape.180.codes
  53.0 121.7 %steps.2 = (bf16[16,16,512]{2,1,0:T(8,128)(2,1)S(1)}, f32[16,16,512]{2,1,0:T(8,128)S(1)}) custom-call(s32[2,64]{1,0:T(2,128)} %reshape.180.codes, s32[2,128]{1,0:T(2,128)} %compare_select_fusion.slots, s32[256]{0:T(256)} %bitcast.29, s32[2,128]{1,0:T(2,128)} %reshape.182.lists, bf16[32,24,128]{2,1,0:T(8,128)(2,1)S(1)} %get-tuple-element.50.coords, ...), custom_call_target="tpu_custom_call" | custom-call | tf_op jit(solution)/shard_map/cond/branch_0_fun/steps/pallas_call | solution.py:541
  174.8 0.7 copy.48
  175.5 0.8 copy.49
  (11 shorter events, 0.1 us)
Async XLA Ops:
  0.7 0.7 copy-start.2
  1.3 0.7 copy-start.4
  4.5 0.7 copy-start.3
  7.0 43.4 %copy-start = (bf16[2,8,16384]{2,1,0:T(8,128)(2,1)S(1)}, bf16[2,8,16384]{2,1,0:T(8,128)(2,1)}, u32[]{:S(2)}) copy-start(bf16[2,8,16384]{2,1,0:T(8,128)(2,1)} %points.1) | copy-start | bytes 1572868
  7.0 43.4 %copy-start.1 = (bf16[2,8,16384]{2,1,0:T(8,128)(2,1)S(1)}, bf16[2,8,16384]{2,1,0:T(8,128)(2,1)}, u32[]{:S(2)}) copy-start(bf16[2,8,16384]{2,1,0:T(8,128)(2,1)} %param.8) | copy-start | bytes 1572868

commit v4 on v3

--- a/solution.py
+++ b/solution.py
@@ -99,6 +99,25 @@
     @pl.when(mine)
     def _():
         pltpu.make_async_copy(src, dst, rsem).start()
+
+
+def pass_around(table, s, y, half, ssem, rsems):
+    above, below = lax.rem(y + 1, PLANES), lax.rem(y + PLANES - 1, PLANES)
+    up = table.at[below, pl.ds(0, half)]
+    drain(up, rsems.at[0])
+    remote(up, up, ssem, rsems.at[4], (s, above)).start()
+    down = table.at[above, pl.ds(half, half)]
+    drain(down, rsems.at[3])
+    remote(down, down, ssem, rsems.at[5], (s, below)).start()
+
+
+def gathered(table, y, half, rsems):
+    above, below = lax.rem(y + 1, PLANES), lax.rem(y + PLANES - 1, PLANES)
+    across = lax.rem(y + 2, PLANES)
+    drain(table.at[below, pl.ds(half, half)], rsems.at[1])
+    drain(table.at[above, pl.ds(0, half)], rsems.at[2])
+    drain(table.at[across, pl.ds(0, half)], rsems.at[4])
+    drain(table.at[across, pl.ds(half, half)], rsems.at[5])
 
 
 def split_blocks(points, step, blocks):
@@ -135,6 +154,7 @@
     r_t,
     s_f,
     r_f,
+    r_g,
 ):
     s = lax.axis_index("strata")
     y = lax.axis_index("comp")
@@ -189,12 +209,20 @@
     def _(k):
         remote(table, tables.at[s // 8], s_t, r_t, (lax.rem(s + 8 * k, owners), y)).start()
 
-    pltpu.make_async_copy(coef, coef_all.at[y], r_c).start()
+    own_copy = pltpu.make_async_copy(coef, coef_all.at[y], r_c)
+    own_copy.start()
     pltpu.make_async_copy(rates, rates_all.at[y], r_r).start()
     for d in range(1, PLANES):
         peer = (s, lax.rem(y + d, PLANES))
-        remote(coef, coef_all.at[y], s_c, r_c, peer).start()
         remote(rates, rates_all.at[y], s_r, r_r, peer).start()
+    half = coef.shape[0] // 2
+    above, below = lax.rem(y + 1, PLANES), lax.rem(y + PLANES - 1, PLANES)
+    low, high = pl.ds(0, half), pl.ds(half, half)
+    for part, at in ((low, 0), (high, 1)):
+        remote(coef.at[part], coef_all.at[y, part], s_c, r_g.at[at], (s, above)).start()
+    for part, at in ((high, 3), (low, 2)):
+        remote(coef.at[part], coef_all.at[y, part], s_c, r_g.at[at], (s, below)).start()
+    pass_around(coef_all, s, y, half, s_c, r_g)
 
     drain(coords, r_p)
     most = coords[0, 16:24, :].astype(jnp.float32)
@@ -208,7 +236,8 @@
     drain(tables.at[pl.ds(0, layers - 1)], s_t)
     drain(full, r_f)
     drain(full.at[pl.ds(0, PLANES - 1)], s_f)
-    drain(coef_all, r_c)
+    own_copy.wait()
+    gathered(coef_all, y, half, r_g)
     drain(rates_all, r_r)
     drain(coef_all.at[pl.ds(0, PLANES - 1)], s_c)
     drain(rates_all.at[pl.ds(0, PLANES - 1)], s_r)
@@ -437,23 +466,33 @@
     end_features(coords1)
     drain(recv0, r_v.at[0])
 
-    def share(q):
-        for d in range(1, PLANES):
-            peer = (s, lax.rem(y + d, PLANES))
-            remote(coef1.at[y, q], coef1.at[y, q], s_c, r_c, peer).start()
-
-    @pl.loop(0, strata_here)
-    def _(q):
-        rounded = refit(q, 0).astype(jnp.bfloat16)
-        middle[q] = rounded
-        coef1[y, q] = rounded
-
-        @pl.when(q > 0)
-        def _():
-            share(q - 1)
-
-    share(strata_here - 1)
-    drain(coef1.at[pl.ds(0, PLANES - 1)], r_c)
+    half = strata_here // 2
+
+    def share(first_q, part):
+        for q in range(2):
+            row = coef1.at[y, first_q + q]
+            above, below = lax.rem(y + 1, PLANES), lax.rem(y + PLANES - 1, PLANES)
+            remote(row, row, s_c, r_c.at[part], (s, above)).start()
+            remote(row, row, s_c, r_c.at[2 + part], (s, below)).start()
+
+    for part in range(2):
+
+        @pl.loop(0, half // 2)
+        def _(g):
+            for h in range(2):
+                q = part * half + 2 * g + h
+                rounded = refit(q, 0).astype(jnp.bfloat16)
+                middle[q] = rounded
+                coef1[y, q] = rounded
+
+            @pl.when(g > 0)
+            def _():
+                share(part * half + 2 * g - 2, part)
+
+        share(part * half + half - 2, part)
+
+    pass_around(coef1, s, y, half, s_c, r_c)
+    gathered(coef1, y, half, r_c)
 
     @pl.loop(0, members)
     def _(j):
@@ -525,7 +564,8 @@
             pltpu.VMEM((points.shape[2] // BLOCK, DIMS, BLOCK), jnp.bfloat16),
             pltpu.VMEM((8, BLOCK), jnp.float32),
         ]
-        + [DMA] * 10,
+        + [DMA] * 10
+        + [DMA((6,))],
         compiler_params=pltpu.CompilerParams(
             collective_id=0, has_side_effects=True, vmem_limit_bytes=LIMIT
         ),
@@ -562,7 +602,7 @@
             pltpu.VMEM((members, 16, BLOCK), bf),
         ]
         + [DMA((STEPS,))] * 5
-        + [DMA] * 4,
+        + [DMA, DMA((6,)), DMA, DMA],
         compiler_params=pltpu.CompilerParams(
             collective_id=room, has_side_effects=True, vmem_limit_bytes=LIMIT
         ),

time: 177 us -> 177 us (level)
  no operation moved by 1% of the time
where the time goes in v4:
time: 177 us; the launch traced here: 176 us
  Pallas kernels  162 us (92%)
  local copies, waits for them, and re-layouts  7.27 us (4%)
  other arithmetic  4.98 us (3%)
  between operations  2.11 us (1%)
    pallas_call x1, Pallas kernels, main(): pl.pallas_call(functools.partial(main_kernel, room), out_shape=(jax.Shape...  121 us
    pallas_call x1, Pallas kernels, exchange(): pl.pallas_call(exchange_kernel, out_shape=(jax.ShapeDtypeStruct((members,...  40.2 us

profile of v4, /device:TPU:1, one launch (start us, length us, event | category | flops | bytes accessed | tf_op | source)
XLA Modules:
  0.0 176.1 jit_solution(6658969489075995398)
XLA Ops:
  0.7 0.0 copy-start.2
  0.7 0.7 copy-done.2
  1.3 0.0 copy-start.4
  1.4 0.6 copy-done.4
  2.0 0.7 broadcast_in_dim.87.rates
  2.7 0.2 convert_reduce_fusion.1
  2.9 0.2 convert_reduce_fusion
  3.1 0.6 select_reduce_fusion.4
  4.4 0.1 select_reduce_fusion.2
  4.5 0.0 copy-start.3
  4.6 0.1 pad.2.clone
  4.6 0.6 copy-done.3
  5.2 0.2 select_reduce_fusion
  5.5 0.6 slice.22
  6.0 0.2 reshape.174
  6.2 0.1 copy.34
  6.3 0.7 maximum_maximum_fusion.table
  7.0 0.0 copy-start
  7.0 0.0 copy-start.1
  7.0 40.2 %exchange.1 = (bf16[32,24,128]{2,1,0:T(8,128)(2,1)S(1)}, bf16[4,16,16,512]{3,2,1,0:T(8,128)(2,1)S(1)}, f32[4,16,128]{2,1,0:T(8,128)S(1)}, bf16[16,8,128]{2,1,0:T(8,128)(2,1)}, f32[4,8,128]{2,1,0:T(8,128)}) custom-call(s32[256]{0:T(256)} %bitcast.28, bf16[2,8,16384]{2,1,0:T(8,128)(2,1)} %points.1, bf16[8,128]{1,0:T(8,128)(2,1)} %maximum_maximum_fusion.table, ...), custom_call_target="tpu_custom_call" | custom-call | tf_op jit(solution)/shard_map/exchange/pallas_call | solution.py:551
  47.2 1.3 slice_reduce_fusion
  49.2 0.1 select_reduce_fusion.3
  49.3 0.1 copy.41
  49.4 0.8 slice_convert_fusion
  50.2 0.1 copy.36
  50.3 0.1 fusion
  50.4 0.0 copy-done
  50.4 0.0 copy-done.1
  50.4 124.1 %conditional.1 = ((bf16[16,16,512]{2,1,0:T(8,128)(2,1)S(1)}, f32[16,16,512]{2,1,0:T(8,128)S(1)})) conditional(s32[]{:T(128)} %convert_element_type.34, (s32[2,128]{1,0:T(2,128)S(1)}, s32[2,128]{1,0:T(2,128)S(1)}, s32[2,128]{1,0:T(2,128)S(1)}, s32[2,256]{1,0:T(2,128)S(1)}, f32[4,16,128]{2,1,0:T(8,128)S(1)}, /*index=5*/s32[2,32,2]{1,2,0:T(2,128)S(1)}, ...), branch_computations={%region_9.10_spmd, %region_10.11_spmd} | conditional | flops 5120 | bytes 12296 | solution.py:678
  50.4 0.6 slice.12
  51.0 0.6 compare_select_fusion.slots
  51.6 0.1 copy.38
  51.7 0.7 reshape.182.lists
  52.3 0.1 copy.37
  52.4 0.7 reshape.180.codes
  53.1 121.4 %steps.2 = (bf16[16,16,512]{2,1,0:T(8,128)(2,1)S(1)}, f32[16,16,512]{2,1,0:T(8,128)S(1)}) custom-call(s32[2,64]{1,0:T(2,128)} %reshape.180.codes, s32[2,128]{1,0:T(2,128)} %compare_select_fusion.slots, s32[256]{0:T(256)} %bitcast.29, s32[2,128]{1,0:T(2,128)} %reshape.182.lists, bf16[32,24,128]{2,1,0:T(8,128)(2,1)S(1)} %get-tuple-element.50.coords, ...), custom_call_target="tpu_custom_call" | custom-call | tf_op jit(solution)/shard_map/cond/branch_0_fun/steps/pallas_call | solution.py:581
  174.6 0.7 copy.48
  175.3 0.8 copy.49
  (11 shorter events, 0.1 us)
Async XLA Ops:
  0.7 0.7 copy-start.2
  1.3 0.7 copy-start.4
  4.5 0.7 copy-start.3
  7.0 43.4 %copy-start = (bf16[2,8,16384]{2,1,0:T(8,128)(2,1)S(1)}, bf16[2,8,16384]{2,1,0:T(8,128)(2,1)}, u32[]{:S(2)}) copy-start(bf16[2,8,16384]{2,1,0:T(8,128)(2,1)} %points.1) | copy-start | bytes 1572868
  7.0 43.4 %copy-start.1 = (bf16[2,8,16384]{2,1,0:T(8,128)(2,1)S(1)}, bf16[2,8,16384]{2,1,0:T(8,128)(2,1)}, u32[]{:S(2)}) copy-start(bf16[2,8,16384]{2,1,0:T(8,128)(2,1)} %param.8) | copy-start | bytes 1572868
